TPU v7x, 768 devices: a whole 4x8x12 slice. The times are simulated.
768 devices in a mesh: dp: 12 (over z_lo, core), tensor: 8 (over z_hi, x), pipe: 8 (over y).
Axes of the slice: x: 4, y: 8, z: 12 (z_hi: 2, z_lo: 6; z = z_hi * 6 + z_lo), core: 2. Of those that a mesh axis runs over, the one named last changes fastest.
Arguments:
- attn_policy: bfloat16 [12, 1024, 4608], P('dp', 'pipe', 'tensor'), may hold values from -0.046875 to 0.046875
- attn_frozen: bfloat16 [12, 1024, 4608], P('dp', 'pipe', 'tensor'), may hold values from -0.046875 to 0.046875
- readout: bfloat16 [12, 1024, 8192], P('dp', 'pipe'), may hold values from -6 to 6
- rest_policy: float32 [12, 1024], P('dp', 'pipe'), may hold values from -3 to 3
- rest_frozen: float32 [12, 1024], P('dp', 'pipe'), may hold values from -3 to 3
- policy_out: bfloat16 [4608, 8192], P('tensor'), may hold values from -0.0625 to 0.0625
- frozen_out: bfloat16 [4608, 8192], P(('tensor', 'dp', 'pipe')), may hold values from -0.0625 to 0.0625
- rewards: float32 [12], replicated, may hold values from -4 to 4
- group_ids: int32 [12], replicated, may hold values from 0 to 5
- prompt_len: int32 [12], replicated, may hold values from 1 to 255
- response_len: int32 [12], replicated, may hold values from 256 to 768
Outputs:
- upstream_grad: bfloat16 [12, 1024, 4608], P('dp', 'pipe', 'tensor')
Inputs may be any that keep to these rules, and one draw needn't show every extreme that they name: `prompt_len`: prompt and response together fit in a rollout.
All inputs are finite; a program needn't handle non-finite values.
Results may differ from a plain program's by a relative error of at most 0.001.
Values may be sent and summed in bfloat16 or wider, within the bound.
No kernel may reach another device: no remote copies, remote signals or barrier semaphores. Data moves between devices by JAX's collectives and lax.ppermute only.
A program may use at most 128 MiB of HBM per device.

v0:
```python
import jax
import jax.numpy as jnp
from jax import lax
from jax.experimental import pallas as pl
from jax.experimental.pallas import tpu as pltpu
from jax.sharding import PartitionSpec as P

KL_WEIGHT = 0.1
AXES = ("dp", "tensor", "pipe")
CORES = 2
SUB = 4
VMEM_BYTES = 16 * 1024 * 1024


def block_sums(items, own, other, sub_mask):
    count = len(items)
    half, width = own.shape
    tokens = CORES * half
    step = width // SUB

    def kernel(*refs):
        mask_ref, own_ref, other_ref, out_ref = refs[2 * count :]
        columns = jnp.concatenate([own_ref[...], other_ref[...]], axis=0)
        rows = jnp.concatenate([r[...] for r in refs[:count]], axis=0)
        view = lax.dot_general(rows, columns, (((1,), (1,)), ((), ())), preferred_element_type=jnp.float32)
        total = jnp.zeros((1, tokens), jnp.float32)
        lo = 0
        for feat_ref in refs[count : 2 * count]:
            n = feat_ref.shape[0]
            kept = feat_ref[...].astype(jnp.float32) * mask_ref[0, :n, :].astype(jnp.float32)
            total += jnp.sum(view[lo : lo + n] * kept, axis=0, keepdims=True)
            lo += n

        @pl.when(pl.program_id(0) == 0)
        def _():
            out_ref[...] = total

        @pl.when(pl.program_id(0) > 0)
        def _():
            out_ref[...] += total

    def whole(array):
        return pl.BlockSpec(array.shape, lambda k: (0, 0))

    most = max(r.shape[0] for r, _ in items)
    rows = sum(r.shape[0] for r, _ in items)
    flat = [r for r, _ in items] + [f for _, f in items]
    specs = [whole(x) for x in flat]
    specs += [
        pl.BlockSpec((1, most, tokens), lambda k: (k, 0, 0)),
        pl.BlockSpec((half, step), lambda k: (0, k)),
        pl.BlockSpec((half, step), lambda k: (0, k)),
    ]
    return pl.pallas_call(
        kernel,
        grid=(SUB,),
        out_shape=jax.ShapeDtypeStruct((1, tokens), jnp.float32),
        in_specs=specs,
        out_specs=pl.BlockSpec((1, tokens), lambda k: (0, 0)),
        cost_estimate=pl.CostEstimate(
            flops=2 * rows * width * tokens, bytes_accessed=rows * step * 2 + 4 * own.size, transcendentals=0
        ),
        compiler_params=pltpu.CompilerParams(
            dimension_semantics=("arbitrary",), vmem_limit_bytes=VMEM_BYTES
        ),
    )(*flat, sub_mask, own, other)


def make(mesh):
    n_dp, n_tensor, n_pipe = (mesh.shape[a] for a in AXES)
    n_z = n_dp // CORES
    half = n_pipe // 2

    def flat(d, t, p):
        return (d * n_tensor + t) * n_pipe + p

    every = [(d, t, p) for d in range(n_dp) for t in range(n_tensor) for p in range(n_pipe)]
    to_partner = [(flat(d, t, p), flat(d ^ 1, t, p)) for d, t, p in every]
    along = [[z * CORES + c for z in range(n_z)] for c in range(CORES)]
    heads = [[(z * CORES + c) * n_tensor + t for c in range(CORES) for t in range(n_tensor)] for z in range(n_z)]

    def partner(array):
        return lax.ppermute(array, AXES, to_partner)

    def shift(array, by):
        return lax.ppermute(array, "pipe", [(i, (i + by) % n_pipe) for i in range(n_pipe)])

    def shards(
        attn_policy,
        attn_frozen,
        readout,
        rest_policy,
        rest_frozen,
        policy_out,
        frozen_out,
        rewards,
        group_ids,
        prompt_len,
        response_len,
    ):
        own = readout[0]
        tokens, width = own.shape
        rows = frozen_out.shape[0]
        step = width // SUB
        core = lax.axis_index("dp") % CORES
        section = lax.axis_index("pipe")
        unit_rows = SUB * rows

        unit = frozen_out.reshape(rows, SUB, step).transpose(1, 0, 2).reshape(unit_rows, step)
        spread = jnp.broadcast_to(unit[None], (n_z, unit_rows, step))
        got_z = lax.all_to_all(spread, "dp", 0, 0, axis_index_groups=along, tiled=True)
        other = partner(own)
        feats = attn_frozen[0].T.reshape(n_z, CORES, n_pipe * rows, tokens)
        mine = lax.dynamic_index_in_dim(feats, core, 1, keepdims=False)
        theirs = lax.dynamic_index_in_dim(feats, 1 - core, 1, keepdims=False)
        theirs = partner(theirs)
        feats = jnp.concatenate([mine, theirs], axis=2).reshape(n_z * n_pipe * rows, CORES * tokens)

        def features(z, y, r):
            source = (z * n_pipe + y) * rows + r
            columns = jnp.arange(n_z * n_pipe * rows, dtype=jnp.int32)
            pick = (source[:, None] == columns[None, :]).astype(jnp.bfloat16)
            return jnp.dot(pick, feats, preferred_element_type=jnp.float32).astype(jnp.bfloat16)

        most = n_z * unit_rows
        at = jnp.arange(n_pipe * most, dtype=jnp.int32)
        y = (section - at // most) % n_pipe
        feats = features(at // unit_rows % n_z, y, at % rows).reshape(n_pipe, most, CORES * tokens)
        feats = [feats[h] for h in range(n_pipe)]
        sub_of_row = jnp.arange(most, dtype=jnp.int32) // rows % SUB
        sub_mask = (sub_of_row[None, :] == jnp.arange(SUB, dtype=jnp.int32)[:, None]).astype(jnp.bfloat16)
        sub_mask = jnp.broadcast_to(sub_mask[:, :, None], (SUB, most, CORES * tokens))

        view_policy = jnp.dot(policy_out, own.T, preferred_element_type=jnp.float32)
        part_policy = jnp.sum(attn_policy[0].T.astype(jnp.float32) * view_policy, axis=0)
        view_policy = shift(view_policy, -1)

        same_group = (group_ids[:, None] == group_ids[None, :]).astype(jnp.float32)
        group_mean = jnp.dot(same_group, rewards, precision=lax.Precision.HIGHEST) / jnp.sum(same_group, axis=1)
        advantage = rewards - group_mean
        chosen = jnp.arange(rewards.shape[0], dtype=jnp.int32) == lax.axis_index("dp")
        adv_one = jnp.sum(jnp.where(chosen, advantage, 0.0))
        start_one = jnp.sum(jnp.where(chosen, prompt_len, 0))
        length_one = jnp.sum(jnp.where(chosen, response_len, 0))
        seq_total = tokens * n_pipe
        positions = section * tokens + jnp.arange(tokens, dtype=jnp.int32)
        inside = (positions >= start_one) & (positions < start_one + length_one)
        weighting = jnp.where(inside, seq_total / length_one.astype(jnp.float32), 0.0)

        block, other, feats, sub_mask, view_policy, part_policy, weighting, adv_one = lax.optimization_barrier(
            (got_z.reshape(most, step), other, feats, sub_mask, view_policy, part_policy, weighting, adv_one)
        )

        def sums(items):
            return block_sums(items, own, other, sub_mask)

        up, down = block, block
        arrived = [(block, feats[0])]
        parts = []
        for hop in range(1, half):
            up = shift(up, 1)
            down = shift(down, -1)
            if hop > 1:
                parts.append(sums(arrived))
                arrived = []
            arrived += [(up, feats[hop]), (down, feats[n_pipe - hop])]
        cut = most // 2
        last_up = shift(up[:cut], 1)
        last_down = shift(down[cut:], -1)
        parts.append(sums(arrived))
        parts.append(sums([(last_up, feats[half][:cut]), (last_down, feats[half][cut:])]))
        total = sum(parts)[0]

        mine, yours = total[:tokens], total[tokens:]
        zero = jnp.zeros_like(mine)
        same = jnp.stack([mine, part_policy])
        cross = jnp.stack([yours, zero])
        by_core = jnp.where(core == 0, jnp.stack([same, cross]), jnp.stack([cross, same]))
        sent = jnp.broadcast_to(by_core[:, None], (CORES, n_tensor, 2, tokens)).reshape(CORES * n_tensor, 2, tokens)
        gathered = lax.all_to_all(sent, ("dp", "tensor"), 0, 0, axis_index_groups=heads, tiled=True)
        summed = gathered.sum(axis=0)
        logp_frozen = rest_frozen[0] + summed[0]
        logp_policy = rest_policy[0] + summed[1]
        slope = weighting * (KL_WEIGHT * (1.0 - jnp.exp(logp_frozen - logp_policy)) - adv_one)
        slope = shift(slope[None], -1)
        token_grad = (slope * view_policy).astype(jnp.bfloat16)
        return token_grad.T[None]

    return shards


def solution(mesh):
    placed = (
        P("dp", "pipe", "tensor"),
        P("dp", "pipe", "tensor"),
        P("dp", "pipe", None),
        P("dp", "pipe"),
        P("dp", "pipe"),
        P("tensor", None),
        P(("tensor", "dp", "pipe"), None),
        P(),
        P(),
        P(),
        P(),
    )
    return jax.shard_map(
        make(mesh), mesh=mesh, in_specs=placed, out_specs=P("dp", "pipe", "tensor"), check_vma=False
    )
```

profile of v0, /device:TPU:1, one launch (start us, length us, event | category | flops | bytes accessed | tf_op | source)
XLA Modules:
  0.0 163.2 jit_solution(7225423451466560214)
XLA Ops:
  0.0 0.9 constant_dynamic-slice_fusion
  0.9 12.4 %collective-permute-start.1 = (bf16[6,48,128]{2,1,0:T(8,128)(2,1)S(1)}, bf16[6,48,128]{2,1,0:T(8,128)(2,1)S(1)}, u32[]{:S(2)}, u32[]{:S(2)}) collective-permute-start(bf16[6,48,128]{2,1,0:T(8,128)(2,1)S(1)} %get-tuple-element.44), channel_id=1, source_target_pairs={{0,64},{1,65},{2,66},{3,67},{4,68},{5,69},{6,70},{7,71},{8,72},{9,... | collective-permute-start | bytes 221192 | tf_op jit(solution)/shard_map/ppermute | solution.py:83
  13.3 0.0 copy-start.9
  13.3 2.1 %collective-permute-start = (bf16[128,8192]{1,0:T(8,128)(2,1)}, bf16[128,8192]{1,0:T(8,128)(2,1)}, u32[]{:S(2)}, u32[]{:S(2)}) collective-permute-start(bf16[128,8192]{1,0:T(8,128)(2,1)} %bitcast.58), channel_id=1, source_target_pairs={{0,64},{1,65},{2,66},{3,67},{4,68},{5,69},{6,70},{7,71},{8,72},{9,... | collective-permute-start | bytes 6291464 | tf_op jit(solution)/shard_map/ppermute | solution.py:83
  15.4 7.6 %fusion.6 = (f32[128]{0:T(128)S(1)}, f32[576,128]{1,0:T(8,128)}) fusion(bf16[1,128,576]{1,2,0:T(8,128)(2,1)} %param.11, bf16[576,8192]{1,0:T(8,128)(2,1)} %param.16, bf16[1,128,8192]{2,1,0:T(8,128)(2,1)} %param.13), kind=kOutput, calls=%fused_computation.10 | convolution fusion | flops 1208180608 | bytes 11977216 | tf_op jit(solution)/shard_map/dot_general | solution.py:134
  23.1 0.0 copy-start.14
  23.1 2.1 %collective-permute-start.2 = (f32[576,128]{1,0:T(8,128)}, f32[576,128]{1,0:T(8,128)S(1)}, u32[]{:S(2)}, u32[]{:S(2)}) collective-permute-start(f32[576,128]{1,0:T(8,128)} %get-tuple-element.50), channel_id=1, source_target_pairs={{0,7},{1,0},{2,1},{3,2},{4,3},{5,4},{6,5},{7,6},{8,15},{9,8},{10,9... | collective-permute-start | bytes 884744 | tf_op jit(solution)/shard_map/ppermute | solution.py:86
  25.1 0.0 copy-done.9
  25.2 0.9 broadcast_in_dim.49
  26.1 6.0 %all-to-all-start = ((bf16[6,24,2048]{2,1,0:T(8,128)(2,1)}), bf16[6,24,2048]{2,1,0:T(8,128)(2,1)S(1)}, u32[]{:S(2)}, u32[]{:S(2)}) async-start(bf16[6,24,2048]{2,1,0:T(8,128)(2,1)} %broadcast_in_dim.49), calls=%async_computation | async-start | bytes 1179648 | tf_op jit(solution)/shard_map/all_to_all | solution.py:111
  32.1 0.0 copy-done.12
  32.1 0.6 select_reduce_fusion
  33.3 0.0 copy-done.13
  33.4 0.7 select_reduce_fusion.1
  35.4 0.0 copy-done.15
  35.4 0.2 fusion.14
  35.6 0.0 copy-done.14
  35.6 0.9 fusion.4
  36.5 0.8 and_select_fusion
  37.3 0.0 collective-permute-done.1
  37.3 0.5 convolution_convert_fusion
  37.8 0.7 fusion.37
  38.5 0.0 collective-permute-done.2
  38.5 16.3 %all-to-all-done = bf16[6,24,2048]{2,1,0:T(8,128)(2,1)S(1)} async-done(((bf16[6,24,2048]{2,1,0:T(8,128)(2,1)}), bf16[6,24,2048]{2,1,0:T(8,128)(2,1)S(1)}, u32[]{:S(2)}, u32[]{:S(2)}) %all-to-all-start) | async-done | bytes 589856 | tf_op jit(solution)/shard_map/all_to_all | solution.py:111
  54.7 0.0 collective-permute-done.refs_8_.refs_6_
  54.7 0.1 broadcast_in_dim.50.refs_6_.refs_4_
  54.9 3.0 %collective-permute-start.4 = (bf16[144,2048]{1,0:T(8,128)(2,1)S(1)}, bf16[144,2048]{1,0:T(8,128)(2,1)S(1)}, u32[]{:S(2)}, u32[]{:S(2)}) collective-permute-start(bf16[144,2048]{1,0:T(8,128)(2,1)S(1)} %bitcast.63), channel_id=1, source_target_pairs={{0,7},{1,0},{2,1},{3,2},{4,3},{5,4},{6,5},{7,6},{8,15},{9,8},{10,9... | collective-permute-start | bytes 1769480 | tf_op jit(solution)/shard_map/ppermute | solution.py:86
  57.9 2.3 %collective-permute-start.3 = (bf16[144,2048]{1,0:T(8,128)(2,1)S(1)}, bf16[144,2048]{1,0:T(8,128)(2,1)S(1)}, u32[]{:S(2)}, u32[]{:S(2)}) collective-permute-start(bf16[144,2048]{1,0:T(8,128)(2,1)S(1)} %bitcast.64), channel_id=1, source_target_pairs={{0,1},{1,2},{2,3},{3,4},{4,5},{5,6},{6,7},{7,0},{8,9},{9,10},{10,1... | collective-permute-start | bytes 1769480 | tf_op jit(solution)/shard_map/ppermute | solution.py:86
  60.2 0.8 copy-done.1
  61.0 9.3 %collective-permute-done.4.refs_2_ = bf16[144,2048]{1,0:T(8,128)(2,1)S(1)} collective-permute-done((bf16[144,2048]{1,0:T(8,128)(2,1)S(1)}, bf16[144,2048]{1,0:T(8,128)(2,1)S(1)}, u32[]{:S(2)}, u32[]{:S(2)}) %collective-permute-start.4) | collective-permute-done | bytes 589856 | tf_op jit(solution)/shard_map/ppermute | solution.py:86
  70.3 4.2 %collective-permute-start.6 = (bf16[144,2048]{1,0:T(8,128)(2,1)S(1)}, bf16[144,2048]{1,0:T(8,128)(2,1)}, u32[]{:S(2)}, u32[]{:S(2)}) collective-permute-start(bf16[144,2048]{1,0:T(8,128)(2,1)S(1)} %collective-permute-done.4.refs_2_), channel_id=1, source_target_pairs={{0,7},{1,0},{2,1},{3,2},{4,3},{5,4},{6,5},{7,6},{8,15},{9,8},{10,9... | collective-permute-start | bytes 1769480 | tf_op jit(solution)/shard_map/ppermute | solution.py:86
  74.5 0.8 copy-done.3
  75.3 0.0 collective-permute-done.3.refs_1_
  75.3 1.9 %collective-permute-start.5 = (bf16[144,2048]{1,0:T(8,128)(2,1)S(1)}, bf16[144,2048]{1,0:T(8,128)(2,1)}, u32[]{:S(2)}, u32[]{:S(2)}) collective-permute-start(bf16[144,2048]{1,0:T(8,128)(2,1)S(1)} %collective-permute-done.3.refs_1_), channel_id=1, source_target_pairs={{0,1},{1,2},{2,3},{3,4},{4,5},{5,6},{6,7},{7,0},{8,9},{9,10},{10,1... | collective-permute-start | bytes 1769480 | tf_op jit(solution)/shard_map/ppermute | solution.py:86
  77.2 0.0 copy-start.5
  77.2 0.8 copy-done.5
  78.1 6.8 %collective-permute-done.6.refs_1_ = bf16[144,2048]{1,0:T(8,128)(2,1)} collective-permute-done((bf16[144,2048]{1,0:T(8,128)(2,1)S(1)}, bf16[144,2048]{1,0:T(8,128)(2,1)}, u32[]{:S(2)}, u32[]{:S(2)}) %collective-permute-start.6) | collective-permute-done | bytes 589856 | tf_op jit(solution)/shard_map/ppermute | solution.py:86
  84.9 5.4 %collective-permute-start.8 = (bf16[144,2048]{1,0:T(8,128)(2,1)}, bf16[144,2048]{1,0:T(8,128)(2,1)S(1)}, u32[]{:S(2)}, u32[]{:S(2)}) collective-permute-start(bf16[144,2048]{1,0:T(8,128)(2,1)} %collective-permute-done.6.refs_1_), channel_id=1, source_target_pairs={{0,7},{1,0},{2,1},{3,2},{4,3},{5,4},{6,5},{7,6},{8,15},{9,8},{10,9... | collective-permute-start | bytes 1769480 | tf_op jit(solution)/shard_map/ppermute | solution.py:86
  90.3 0.5 collective-permute-done.5.refs_0_
  90.8 1.9 %collective-permute-start.7 = (bf16[144,2048]{1,0:T(8,128)(2,1)}, bf16[144,2048]{1,0:T(8,128)(2,1)}, u32[]{:S(2)}, u32[]{:S(2)}) collective-permute-start(bf16[144,2048]{1,0:T(8,128)(2,1)} %collective-permute-done.5.refs_0_), channel_id=1, source_target_pairs={{0,1},{1,2},{2,3},{3,4},{4,5},{5,6},{6,7},{7,0},{8,9},{9,10},{10,1... | collective-permute-start | bytes 1769480 | tf_op jit(solution)/shard_map/ppermute | solution.py:86
  92.8 0.8 fusion.38
  93.6 6.6 %collective-permute-done.8.refs_1_ = bf16[144,2048]{1,0:T(8,128)(2,1)S(1)} collective-permute-done((bf16[144,2048]{1,0:T(8,128)(2,1)}, bf16[144,2048]{1,0:T(8,128)(2,1)S(1)}, u32[]{:S(2)}, u32[]{:S(2)}) %collective-permute-start.8) | collective-permute-done | bytes 589856 | tf_op jit(solution)/shard_map/ppermute | solution.py:86
  100.2 5.2 %collective-permute-start.10 = (bf16[72,2048]{1,0:T(8,128)(2,1)S(1)}, bf16[72,2048]{1,0:T(8,128)(2,1)S(1)}, u32[]{:S(2)}, u32[]{:S(2)}) collective-permute-start(bf16[72,2048]{1,0:T(8,128)(2,1)S(1)} %slice.83), channel_id=1, source_target_pairs={{0,7},{1,0},{2,1},{3,2},{4,3},{5,4},{6,5},{7,6},{8,15},{9,8},{10,9... | collective-permute-start | bytes 884744 | tf_op jit(solution)/shard_map/ppermute | solution.py:86
  105.4 0.3 collective-permute-done.7.refs_0_
  105.7 1.0 slice.82
  106.7 1.9 %collective-permute-start.9 = (bf16[72,2048]{1,0:T(8,128)(2,1)S(1)}, bf16[72,2048]{1,0:T(8,128)(2,1)S(1)}, u32[]{:S(2)}, u32[]{:S(2)}) collective-permute-start(bf16[72,2048]{1,0:T(8,128)(2,1)S(1)} %slice.82), channel_id=1, source_target_pairs={{0,1},{1,2},{2,3},{3,4},{4,5},{5,6},{6,7},{7,0},{8,9},{9,10},{10,1... | collective-permute-start | bytes 884744 | tf_op jit(solution)/shard_map/ppermute | solution.py:86
  108.7 0.0 copy-done
  108.7 0.0 copy-start.2
  108.7 1.1 copy-done.2
  109.7 1.1 copy-done.4
  110.8 1.1 copy-done.6
  111.9 4.3 %shard_map.109 = f32[1,256]{1,0:T(1,128)S(1)} custom-call(bf16[144,2048]{1,0:T(8,128)(2,1)S(1)} %bitcast.65, bf16[144,2048]{1,0:T(8,128)(2,1)S(1)} %copy-done.6, bf16[144,2048]{1,0:T(8,128)(2,1)S(1)} %copy-done.4, bf16[144,256]{1,0:T(8,128)(2,1)S(1)} %get-tuple-element.22.refs_3_, bf16[144,256]{1,0:T(8,128)(2,1)S(1)} %get-tuple-element.23.refs_4_, ...), custom_call_target="tpu_custom_call" | custom-call | flops 1811939328 | bytes 5963776 | tf_op jit(solution)/shard_map/pallas_call | solution.py:54
  116.2 4.2 %shard_map.110 = f32[1,256]{1,0:T(1,128)S(1)} custom-call(bf16[144,2048]{1,0:T(8,128)(2,1)} %collective-permute-done.5.refs_0_, bf16[144,2048]{1,0:T(8,128)(2,1)} %collective-permute-done.6.refs_1_, bf16[144,256]{1,0:T(8,128)(2,1)S(1)} %get-tuple-element.27.refs_2_, bf16[144,256]{1,0:T(8,128)(2,1)S(1)} %get-tuple-element.28.refs_3_, ...), custom_call_target="tpu_custom_call" | custom-call | flops 1207959552 | bytes 5373952 | tf_op jit(solution)/shard_map/pallas_call | solution.py:54
  120.4 4.0 %shard_map.111 = f32[1,256]{1,0:T(1,128)S(1)} custom-call(bf16[144,2048]{1,0:T(8,128)(2,1)} %collective-permute-done.7.refs_0_, bf16[144,2048]{1,0:T(8,128)(2,1)S(1)} %collective-permute-done.8.refs_1_, bf16[144,256]{1,0:T(8,128)(2,1)S(1)} %get-tuple-element.29.refs_2_, bf16[144,256]{1,0:T(8,128)(2,1)S(1)} %get-tuple-element.30.refs_3_, ...), custom_call_target="tpu_custom_call" | custom-call | flops 1207959552 | bytes 5373952 | tf_op jit(solution)/shard_map/pallas_call | solution.py:54
  124.4 0.0 collective-permute-done.10.refs_1_
  124.4 0.0 collective-permute-done.9.refs_0_
  124.5 0.0 copy-start.10
  124.5 0.0 copy-start.11
  124.5 3.8 %shard_map.112 = f32[1,256]{1,0:T(1,128)S(1)} custom-call(bf16[72,2048]{1,0:T(8,128)(2,1)S(1)} %collective-permute-done.9.refs_0_, bf16[72,2048]{1,0:T(8,128)(2,1)S(1)} %collective-permute-done.10.refs_1_, bf16[72,256]{1,0:T(8,128)(2,1)S(1)} %get-tuple-element.46.refs_2_, bf16[72,256]{1,0:T(8,128)(2,1)S(1)} %get-tuple-element.45.refs_3_, ...), custom_call_target="tpu_custom_call" | custom-call | flops 603979776 | bytes 4784128 | tf_op jit(solution)/shard_map/pallas_call | solution.py:54
  128.4 27.8 %all_to_all.10 = f32[16,2,128]{2,1,0:T(2,128)S(1)} all-to-all(f32[16,2,128]{2,1,0:T(2,128)S(1)} %bitcast.69), channel_id=1, replica_groups={{0,8,16,24,32,40,48,56,64,72,80,88,96,104,112,120},{128,136,144,152,160..., dimensions={0} | all-to-all | bytes 32768 | tf_op jit(solution)/shard_map/all_to_all | solution.py:180
  156.3 0.6 fusion.32
  156.9 4.9 %collective-permute-start.11 = (f32[1,128]{1,0:T(1,128)S(1)}, f32[1,128]{1,0:T(1,128)S(1)}, u32[]{:S(2)}, u32[]{:S(2)}) collective-permute-start(f32[1,128]{1,0:T(1,128)S(1)} %fusion.32), channel_id=1, source_target_pairs={{0,7},{1,0},{2,1},{3,2},{4,3},{5,4},{6,5},{7,6},{8,15},{9,8},{10,9... | collective-permute-start | bytes 1544 | tf_op jit(solution)/shard_map/ppermute | solution.py:86
  161.8 0.7 collective-permute-done.11
  162.5 0.7 fusion.7
  (25 shorter events, 0.2 us)
Async XLA Ops:
  0.9 36.3 %collective-permute-start.1 = (bf16[6,48,128]{2,1,0:T(8,128)(2,1)S(1)}, bf16[6,48,128]{2,1,0:T(8,128)(2,1)S(1)}, u32[]{:S(2)}, u32[]{:S(2)}) collective-permute-start(bf16[6,48,128]{2,1,0:T(8,128)(2,1)S(1)} %get-tuple-element.44), channel_id=1, source_target_pairs={{0,64},{1,65},{2,66},{3,67},{4,68},{5,69},{6,70},{7,71},{8,72},{9,... | collective-permute-start | bytes 221192 | tf_op jit(solution)/shard_map/ppermute | solution.py:83
  13.3 11.8 %copy-start.9 = (bf16[6,8192]{1,0:T(8,128)(2,1)S(1)}, bf16[6,8192]{1,0:T(8,128)(2,1)}, u32[]{:S(2)}) copy-start(bf16[6,8192]{1,0:T(8,128)(2,1)} %param.17) | copy-start | bytes 294916
  13.3 41.4 %collective-permute-start = (bf16[128,8192]{1,0:T(8,128)(2,1)}, bf16[128,8192]{1,0:T(8,128)(2,1)}, u32[]{:S(2)}, u32[]{:S(2)}) collective-permute-start(bf16[128,8192]{1,0:T(8,128)(2,1)} %bitcast.58), channel_id=1, source_target_pairs={{0,64},{1,65},{2,66},{3,67},{4,68},{5,69},{6,70},{7,71},{8,72},{9,... | collective-permute-start | bytes 6291464 | tf_op jit(solution)/shard_map/ppermute | solution.py:83
  23.1 9.0 %copy-start.12 = (s32[12]{0:T(128)S(1)}, s32[12]{0:T(128)}, u32[]{:S(2)}) copy-start(s32[12]{0:T(128)} %param.21) | copy-start | bytes 148
  23.1 10.3 %copy-start.13 = (s32[12]{0:T(128)S(1)}, s32[12]{0:T(128)}, u32[]{:S(2)}) copy-start(s32[12]{0:T(128)} %param.20) | copy-start | bytes 148
  23.1 12.4 %copy-start.15 = (s32[12]{0:T(128)S(1)}, s32[12]{0:T(128)}, u32[]{:S(2)}) copy-start(s32[12]{0:T(128)} %param.19) | copy-start | bytes 148
  23.1 12.5 %copy-start.14 = (f32[12]{0:T(128)S(1)}, f32[12]{0:T(128)}, u32[]{:S(2)}) copy-start(f32[12]{0:T(128)} %param.18) | copy-start | bytes 148
  23.1 15.4 %collective-permute-start.2 = (f32[576,128]{1,0:T(8,128)}, f32[576,128]{1,0:T(8,128)S(1)}, u32[]{:S(2)}, u32[]{:S(2)}) collective-permute-start(f32[576,128]{1,0:T(8,128)} %get-tuple-element.50), channel_id=1, source_target_pairs={{0,7},{1,0},{2,1},{3,2},{4,3},{5,4},{6,5},{7,6},{8,15},{9,8},{10,9... | collective-permute-start | bytes 884744 | tf_op jit(solution)/shard_map/ppermute | solution.py:86
  26.1 28.7 %all-to-all-start = ((bf16[6,24,2048]{2,1,0:T(8,128)(2,1)}), bf16[6,24,2048]{2,1,0:T(8,128)(2,1)S(1)}, u32[]{:S(2)}, u32[]{:S(2)}) async-start(bf16[6,24,2048]{2,1,0:T(8,128)(2,1)} %broadcast_in_dim.49), calls=%async_computation | async-start | bytes 1179648 | tf_op jit(solution)/shard_map/all_to_all | solution.py:111
  36.5 72.2 %copy-start = (bf16[1,128,8192]{2,1,0:T(8,128)(2,1)S(1)}, bf16[1,128,8192]{2,1,0:T(8,128)(2,1)}, u32[]{:S(2)}) copy-start(bf16[1,128,8192]{2,1,0:T(8,128)(2,1)} %param.13) | copy-start | bytes 6291460
  38.5 16.3 %copy-start.7 = (f32[576,128]{1,0:T(8,128)}, f32[576,128]{1,0:T(8,128)S(1)}, u32[]{:S(2)}) copy-start(f32[576,128]{1,0:T(8,128)S(1)} %collective-permute-done.2) | copy-start | bytes 884740
  54.9 15.4 %collective-permute-start.4 = (bf16[144,2048]{1,0:T(8,128)(2,1)S(1)}, bf16[144,2048]{1,0:T(8,128)(2,1)S(1)}, u32[]{:S(2)}, u32[]{:S(2)}) collective-permute-start(bf16[144,2048]{1,0:T(8,128)(2,1)S(1)} %bitcast.63), channel_id=1, source_target_pairs={{0,7},{1,0},{2,1},{3,2},{4,3},{5,4},{6,5},{7,6},{8,15},{9,8},{10,9... | collective-permute-start | bytes 1769480 | tf_op jit(solution)/shard_map/ppermute | solution.py:86
  57.9 17.4 %collective-permute-start.3 = (bf16[144,2048]{1,0:T(8,128)(2,1)S(1)}, bf16[144,2048]{1,0:T(8,128)(2,1)S(1)}, u32[]{:S(2)}, u32[]{:S(2)}) collective-permute-start(bf16[144,2048]{1,0:T(8,128)(2,1)S(1)} %bitcast.64), channel_id=1, source_target_pairs={{0,1},{1,2},{2,3},{3,4},{4,5},{5,6},{6,7},{7,0},{8,9},{9,10},{10,1... | collective-permute-start | bytes 1769480 | tf_op jit(solution)/shard_map/ppermute | solution.py:86
  60.2 0.8 copy-start.1
  70.3 14.6 %collective-permute-start.6 = (bf16[144,2048]{1,0:T(8,128)(2,1)S(1)}, bf16[144,2048]{1,0:T(8,128)(2,1)}, u32[]{:S(2)}, u32[]{:S(2)}) collective-permute-start(bf16[144,2048]{1,0:T(8,128)(2,1)S(1)} %collective-permute-done.4.refs_2_), channel_id=1, source_target_pairs={{0,7},{1,0},{2,1},{3,2},{4,3},{5,4},{6,5},{7,6},{8,15},{9,8},{10,9... | collective-permute-start | bytes 1769480 | tf_op jit(solution)/shard_map/ppermute | solution.py:86
  74.5 0.8 copy-start.3
  75.3 15.6 %collective-permute-start.5 = (bf16[144,2048]{1,0:T(8,128)(2,1)S(1)}, bf16[144,2048]{1,0:T(8,128)(2,1)}, u32[]{:S(2)}, u32[]{:S(2)}) collective-permute-start(bf16[144,2048]{1,0:T(8,128)(2,1)S(1)} %collective-permute-done.3.refs_1_), channel_id=1, source_target_pairs={{0,1},{1,2},{2,3},{3,4},{4,5},{5,6},{6,7},{7,0},{8,9},{9,10},{10,1... | collective-permute-start | bytes 1769480 | tf_op jit(solution)/shard_map/ppermute | solution.py:86
  77.2 0.9 copy-start.5
  84.9 15.3 %collective-permute-start.8 = (bf16[144,2048]{1,0:T(8,128)(2,1)}, bf16[144,2048]{1,0:T(8,128)(2,1)S(1)}, u32[]{:S(2)}, u32[]{:S(2)}) collective-permute-start(bf16[144,2048]{1,0:T(8,128)(2,1)} %collective-permute-done.6.refs_1_), channel_id=1, source_target_pairs={{0,7},{1,0},{2,1},{3,2},{4,3},{5,4},{6,5},{7,6},{8,15},{9,8},{10,9... | collective-permute-start | bytes 1769480 | tf_op jit(solution)/shard_map/ppermute | solution.py:86
  90.8 14.9 %collective-permute-start.7 = (bf16[144,2048]{1,0:T(8,128)(2,1)}, bf16[144,2048]{1,0:T(8,128)(2,1)}, u32[]{:S(2)}, u32[]{:S(2)}) collective-permute-start(bf16[144,2048]{1,0:T(8,128)(2,1)} %collective-permute-done.5.refs_0_), channel_id=1, source_target_pairs={{0,1},{1,2},{2,3},{3,4},{4,5},{5,6},{6,7},{7,0},{8,9},{9,10},{10,1... | collective-permute-start | bytes 1769480 | tf_op jit(solution)/shard_map/ppermute | solution.py:86
  100.2 24.2 %collective-permute-start.10 = (bf16[72,2048]{1,0:T(8,128)(2,1)S(1)}, bf16[72,2048]{1,0:T(8,128)(2,1)S(1)}, u32[]{:S(2)}, u32[]{:S(2)}) collective-permute-start(bf16[72,2048]{1,0:T(8,128)(2,1)S(1)} %slice.83), channel_id=1, source_target_pairs={{0,7},{1,0},{2,1},{3,2},{4,3},{5,4},{6,5},{7,6},{8,15},{9,8},{10,9... | collective-permute-start | bytes 884744 | tf_op jit(solution)/shard_map/ppermute | solution.py:86
  106.7 17.7 %collective-permute-start.9 = (bf16[72,2048]{1,0:T(8,128)(2,1)S(1)}, bf16[72,2048]{1,0:T(8,128)(2,1)S(1)}, u32[]{:S(2)}, u32[]{:S(2)}) collective-permute-start(bf16[72,2048]{1,0:T(8,128)(2,1)S(1)} %slice.82), channel_id=1, source_target_pairs={{0,1},{1,2},{2,3},{3,4},{4,5},{5,6},{6,7},{7,0},{8,9},{9,10},{10,1... | collective-permute-start | bytes 884744 | tf_op jit(solution)/shard_map/ppermute | solution.py:86
  108.7 1.1 copy-start.2
  109.7 1.1 copy-start.4
  110.8 1.1 copy-start.6
  124.5 31.8 %copy-start.10 = (f32[1,128]{1,0:T(1,128)S(1)}, f32[1,128]{1,0:T(1,128)}, u32[]{:S(2)}) copy-start(f32[1,128]{1,0:T(1,128)} %param.14) | copy-start | bytes 1540
  124.5 31.8 %copy-start.11 = (f32[1,128]{1,0:T(1,128)S(1)}, f32[1,128]{1,0:T(1,128)}, u32[]{:S(2)}) copy-start(f32[1,128]{1,0:T(1,128)} %param.15) | copy-start | bytes 1540
  124.5 38.0 %copy-start.8 = (f32[576,128]{1,0:T(8,128)S(1)}, f32[576,128]{1,0:T(8,128)}, u32[]{:S(2)}) copy-start(f32[576,128]{1,0:T(8,128)} %copy-done.7) | copy-start | bytes 884740
  156.9 5.6 %collective-permute-start.11 = (f32[1,128]{1,0:T(1,128)S(1)}, f32[1,128]{1,0:T(1,128)S(1)}, u32[]{:S(2)}, u32[]{:S(2)}) collective-permute-start(f32[1,128]{1,0:T(1,128)S(1)} %fusion.32), channel_id=1, source_target_pairs={{0,7},{1,0},{2,1},{3,2},{4,3},{5,4},{6,5},{7,6},{8,15},{9,8},{10,9... | collective-permute-start | bytes 1544 | tf_op jit(solution)/shard_map/ppermute | solution.py:86
where the time goes:
time: 164 us; the launch traced here: 163 us
  starting transfers between devices  53.2 us (32%)
  waiting for transfers between devices  40.6 us (25%)
  blocking collectives  27.8 us (17%)
  Pallas kernels  16.4 us (10%)
  local copies, waits for them, and re-layouts  10.2 us (6%)
  matrix products  9.03 us (6%)
  other arithmetic  3.68 us (2%)
  between operations  2.37 us (1%)
    ppermute x10, starting transfers between devices, shift(): lax.ppermute(array, 'pipe', [(i, (i + by) % n_pipe) for i in range(n_pipe)])  32.7 us
    all_to_all x1, blocking collectives, shards(): lax.all_to_all(sent, ('dp', 'tensor'), 0, 0, axis_index_groups=heads, til...  27.8 us
    ppermute x10, waiting for transfers between devices, shift(): lax.ppermute(array, 'pipe', [(i, (i + by) % n_pipe) for i in range(n_pipe)])  24.3 us
    pallas_call x4, Pallas kernels, block_sums(): pl.pallas_call(kernel, grid=(SUB,), out_shape=jax.ShapeDtypeStruct((1, to...  16.4 us
    all_to_all x1, waiting for transfers between devices, shards(): lax.all_to_all(spread, 'dp', 0, 0, axis_index_groups=along, tiled=True)  16.3 us
    ppermute x2, starting transfers between devices, partner(): return lax.ppermute(array, AXES, to_partner)  14.4 us
    dot_general x1, matrix products, shards(): view_policy = jnp.dot(policy_out, own.T, preferred_element_type=jnp.float32)  7.65 us
    all_to_all x1, starting transfers between devices, shards(): lax.all_to_all(spread, 'dp', 0, 0, axis_index_groups=along, tiled=True)  6 us
  transfers between devices with their start and end apart: 13, of which 7 were waited for; matrix products, arithmetic and copies ran while one was open for 9% of the time, Pallas kernels for 8%

commit v1 on v0

v1 whole, which is shorter than its diff:
```python
import jax
import jax.numpy as jnp
from jax import lax
from jax.experimental import pallas as pl
from jax.experimental.pallas import tpu as pltpu
from jax.sharding import PartitionSpec as P

KL_WEIGHT = 0.1
AXES = ("dp", "tensor", "pipe")
MEMBERS = 4
SUB = 4
MASK_ROWS = 48
STEPS = 2
VMEM_BYTES = 24 * 1024 * 1024


def block_sums(items, feats, seen, sub_mask):
    count = len(items)
    tokens = seen.shape[0]
    step = items[0][0].shape[1]

    def kernel(*refs):
        mask_ref, seen_ref, out_ref = refs[2 * count :]
        total = jnp.zeros((1, tokens), jnp.float32)
        for k in range(SUB // STEPS):
            terms = jnp.zeros((MASK_ROWS, tokens), jnp.float32)
            for row_ref, feat_ref in zip(refs[:count], refs[count : 2 * count]):
                view = lax.dot_general(
                    row_ref[...],
                    seen_ref[:, k * step : (k + 1) * step],
                    (((1,), (1,)), ((), ())),
                    preferred_element_type=jnp.float32,
                )
                for at in range(0, row_ref.shape[0], MASK_ROWS):
                    terms += view[at : at + MASK_ROWS] * feat_ref[0, at : at + MASK_ROWS, :].astype(jnp.float32)
            total += jnp.sum(terms * mask_ref[k].astype(jnp.float32), axis=0, keepdims=True)

        @pl.when(pl.program_id(0) == 0)
        def _():
            out_ref[...] = total

        @pl.when(pl.program_id(0) > 0)
        def _():
            out_ref[...] += total

    blocks = [r for r, _ in items]
    rows = sum(r.shape[0] for r, _ in items)
    specs = [pl.BlockSpec(x.shape, lambda k: (0, 0)) for x in blocks]
    specs += [pl.BlockSpec((1, *feats.shape[1:]), lambda k, at=at: (at, 0, 0)) for _, at in items]
    specs += [
        pl.BlockSpec((SUB // STEPS, MASK_ROWS, tokens), lambda k: (k, 0, 0)),
        pl.BlockSpec((tokens, step * SUB // STEPS), lambda k: (0, k)),
    ]
    return pl.pallas_call(
        kernel,
        grid=(STEPS,),
        out_shape=jax.ShapeDtypeStruct((1, tokens), jnp.float32),
        in_specs=specs,
        out_specs=pl.BlockSpec((1, tokens), lambda k: (0, 0)),
        cost_estimate=pl.CostEstimate(
            flops=2 * rows * SUB * step * tokens, bytes_accessed=rows * step * 2 + 2 * seen.size, transcendentals=0
        ),
        compiler_params=pltpu.CompilerParams(dimension_semantics=("arbitrary",), vmem_limit_bytes=VMEM_BYTES),
    )(*blocks, *[feats] * count, sub_mask, seen)


def column_parts(array, count):
    rows, width = array.shape
    part = width // count

    def kernel(in_ref, out_ref):
        out_ref[0] = in_ref[...]

    return pl.pallas_call(
        kernel,
        grid=(count,),
        out_shape=jax.ShapeDtypeStruct((count, rows, part), array.dtype),
        in_specs=[pl.BlockSpec((rows, part), lambda m: (0, m))],
        out_specs=pl.BlockSpec((1, rows, part), lambda m: (m, 0, 0)),
        cost_estimate=pl.CostEstimate(flops=0, bytes_accessed=4 * array.size, transcendentals=0),
        compiler_params=pltpu.CompilerParams(dimension_semantics=("arbitrary",), vmem_limit_bytes=VMEM_BYTES),
    )(array)


def in_hbm(array):
    return pltpu.with_memory_space_constraint(array, pltpu.HBM)


def make(mesh):
    n_dp, n_tensor, n_pipe = (mesh.shape[a] for a in AXES)
    half = n_pipe // 2
    groups = [list(range(lo, lo + MEMBERS)) for lo in range(0, n_dp, MEMBERS)]
    heads = [[d * n_tensor + t for d in group for t in range(n_tensor)] for group in groups]

    def shift(array, by):
        return lax.ppermute(array, "pipe", [(i, (i + by) % n_pipe) for i in range(n_pipe)])

    def shards(
        attn_policy,
        attn_frozen,
        readout,
        rest_policy,
        rest_frozen,
        policy_out,
        frozen_out,
        rewards,
        group_ids,
        prompt_len,
        response_len,
    ):
        own = readout[0]
        tokens, width = own.shape
        rows = frozen_out.shape[0]
        quarter = width // MEMBERS
        step = quarter // SUB
        member = lax.axis_index("dp") % MEMBERS
        section = lax.axis_index("pipe")
        unit_rows = SUB * rows
        block_rows = n_dp * unit_rows
        shared = MEMBERS * tokens

        parts = frozen_out.reshape(rows, MEMBERS, SUB, step).transpose(1, 2, 0, 3).reshape(MEMBERS, unit_rows, step)
        parts = jnp.broadcast_to(parts[None], (n_dp // MEMBERS, MEMBERS, unit_rows, step))
        block = lax.all_to_all(parts.reshape(n_dp, unit_rows, step), "dp", 0, 0, tiled=True)
        block = block.reshape(block_rows, step)

        split = column_parts(own, MEMBERS)
        seen = lax.all_to_all(split, "dp", 0, 0, axis_index_groups=groups, tiled=True).reshape(shared, quarter)
        seen = in_hbm(seen)

        view_policy = jnp.dot(policy_out, own.T, preferred_element_type=jnp.float32)
        part_policy = jnp.sum(attn_policy[0].T.astype(jnp.float32) * view_policy, axis=0)

        feats = attn_frozen[0].T
        for bit in (1, 2):
            theirs = lax.ppermute(feats, "dp", [(d, d ^ bit) for d in range(n_dp)])
            if bit == 2:
                block, view_policy, part_policy, theirs = lax.optimization_barrier(
                    (block, view_policy, part_policy, theirs)
                )
            second = (member & bit) != 0
            feats = jnp.concatenate(
                [jnp.where(second, theirs, feats), jnp.where(second, feats, theirs)], axis=1
            )
        at = jnp.arange(n_pipe * block_rows, dtype=jnp.int32)
        source = at // unit_rows % n_dp * n_pipe + (section - at // block_rows) % n_pipe
        source = source * rows + at % rows
        columns = jnp.arange(n_dp * n_pipe * rows, dtype=jnp.int32)
        pick = (source[:, None] == columns[None, :]).astype(jnp.bfloat16)
        feats = jnp.dot(pick, feats, preferred_element_type=jnp.float32).astype(jnp.bfloat16)
        feats = in_hbm(feats.reshape(n_pipe, block_rows, shared))
        sub_of_row = jnp.arange(MASK_ROWS, dtype=jnp.int32) // rows % SUB
        sub_mask = (sub_of_row[None, :] == jnp.arange(SUB, dtype=jnp.int32)[:, None]).astype(jnp.bfloat16)
        sub_mask = jnp.broadcast_to(sub_mask[:, :, None], (SUB, MASK_ROWS, shared))

        def sums(items):
            return block_sums(items, feats, seen, sub_mask)

        up, down = block, block
        arrived = [[(block, 0)]]
        for hop in range(1, half):
            up = shift(up, 1)
            down = shift(down, -1)
            arrived.append([(up, hop), (down, n_pipe - hop)])
        last = shift(up, 1)
        total = sums(arrived[0] + arrived[1] + arrived[2] + arrived[3])
        total += sums([(last, half)])

        frozen = total.reshape(MEMBERS, 1, tokens)
        me = jnp.arange(MEMBERS, dtype=jnp.int32)[:, None, None] == member
        policy = jnp.where(me, part_policy[None, None, :], 0.0)
        sent = jnp.concatenate([frozen, policy], axis=1)
        sent = jnp.broadcast_to(sent[:, None], (MEMBERS, n_tensor, 2, tokens)).reshape(MEMBERS * n_tensor, 2, tokens)
        sent, rewards, group_ids, prompt_len, response_len = lax.optimization_barrier(
            (sent, rewards, group_ids, prompt_len, response_len)
        )
        gathered = lax.all_to_all(sent, ("dp", "tensor"), 0, 0, axis_index_groups=heads, tiled=True)
        summed = gathered.sum(axis=0)

        same_group = (group_ids[:, None] == group_ids[None, :]).astype(jnp.float32)
        group_mean = jnp.dot(same_group, rewards, precision=lax.Precision.HIGHEST) / jnp.sum(same_group, axis=1)
        advantage = rewards - group_mean
        chosen = jnp.arange(rewards.shape[0], dtype=jnp.int32) == lax.axis_index("dp")
        adv_one = jnp.sum(jnp.where(chosen, advantage, 0.0))
        start_one = jnp.sum(jnp.where(chosen, prompt_len, 0))
        length_one = jnp.sum(jnp.where(chosen, response_len, 0))
        seq_total = tokens * n_pipe
        positions = section * tokens + jnp.arange(tokens, dtype=jnp.int32)
        inside = (positions >= start_one) & (positions < start_one + length_one)
        weighting = jnp.where(inside, seq_total / length_one.astype(jnp.float32), 0.0)

        logp_frozen = rest_frozen[0] + summed[0]
        logp_policy = rest_policy[0] + summed[1]
        slope = weighting * (KL_WEIGHT * (1.0 - jnp.exp(logp_frozen - logp_policy)) - adv_one)
        view_policy = shift(view_policy, -1)
        slope = shift(slope[None], -1)
        token_grad = (slope * view_policy).astype(jnp.bfloat16)
        return token_grad.T[None]

    return shards


def solution(mesh):
    placed = (
        P("dp", "pipe", "tensor"),
        P("dp", "pipe", "tensor"),
        P("dp", "pipe", None),
        P("dp", "pipe"),
        P("dp", "pipe"),
        P("tensor", None),
        P(("tensor", "dp", "pipe"), None),
        P(),
        P(),
        P(),
        P(),
    )
    return jax.shard_map(
        make(mesh), mesh=mesh, in_specs=placed, out_specs=P("dp", "pipe", "tensor"), check_vma=False
    )
```

time: 164 us -> 154 us (0.939)
  the two profiles are of different devices: /device:TPU:1 before, /device:TPU:24 now
where the time goes in v1:
time: 154 us; the launch traced here: 153 us
  starting transfers between devices  66.7 us (43%)
  waiting for transfers between devices  54.6 us (35%)
  matrix products  11.4 us (7%)
  Pallas kernels  11 us (7%)
  local copies, waits for them, and re-layouts  4.21 us (3%)
  other arithmetic  3.09 us (2%)
  between operations  2.27 us (1%)
    ppermute x9, starting transfers between devices, shift(): lax.ppermute(array, 'pipe', [(i, (i + by) % n_pipe) for i in range(n_pipe)])  31.1 us
    ppermute x2, waiting for transfers between devices, shards(): theirs = lax.ppermute(feats, 'dp', [(d, d ^ bit) for d in range(n_dp)])  18.7 us
    ppermute x9, waiting for transfers between devices, shift(): lax.ppermute(array, 'pipe', [(i, (i + by) % n_pipe) for i in range(n_pipe)])  13.1 us
    all_to_all x1, starting transfers between devices, shards(): lax.all_to_all(sent, ('dp', 'tensor'), 0, 0, axis_index_groups=heads, til...  13 us
    all_to_all x1, starting transfers between devices, shards(): lax.all_to_all(parts.reshape(n_dp, unit_rows, step), 'dp', 0, 0, tiled=True)  12.1 us
    all_to_all x1, waiting for transfers between devices, shards(): lax.all_to_all(parts.reshape(n_dp, unit_rows, step), 'dp', 0, 0, tiled=True)  11.4 us
    all_to_all x1, waiting for transfers between devices, shards(): lax.all_to_all(sent, ('dp', 'tensor'), 0, 0, axis_index_groups=heads, til...  11.4 us
    pallas_call x2, Pallas kernels, block_sums(): pl.pallas_call(kernel, grid=(STEPS,), out_shape=jax.ShapeDtypeStruct((1,...  9.06 us
  transfers between devices with their start and end apart: 14, of which 9 were waited for; matrix products, arithmetic and copies ran while one was open for 9% of the time, Pallas kernels for 7%

profile of v1, /device:TPU:24, one launch (start us, length us, event | category | flops | bytes accessed | tf_op | source)
XLA Modules:
  0.0 153.3 jit_solution(7852668977244370213)
XLA Ops:
  0.0 1.1 reshape.190
  1.1 0.7 broadcast_in_dim.71
  1.9 12.1 %all-to-all-start = ((bf16[12,24,512]{2,1,0:T(8,128)(2,1)}), bf16[12,24,512]{2,1,0:T(8,128)(2,1)S(1)}, u32[]{:S(2)}, u32[]{:S(2)}) async-start(bf16[12,24,512]{2,1,0:T(8,128)(2,1)} %bitcast.2), calls=%async_computation | async-start | bytes 589824 | tf_op jit(solution)/shard_map/all_to_all | solution.py:124
  14.0 0.0 copy-start
  14.0 1.6 %copy-done = bf16[1,128,8192]{2,1,0:T(8,128)(2,1)S(1)} copy-done((bf16[1,128,8192]{2,1,0:T(8,128)(2,1)S(1)}, bf16[1,128,8192]{2,1,0:T(8,128)(2,1)}, u32[]{:S(2)}) %copy-start) | copy-done | bytes 2097176
  15.6 2.0 %shard_map.109 = bf16[4,128,2048]{2,1,0:T(8,128)(2,1)} custom-call(bf16[128,8192]{1,0:T(8,128)(2,1)S(1)} %bitcast.47), custom_call_target="tpu_custom_call" | custom-call | bytes 4194304 | tf_op jit(solution)/shard_map/pallas_call | solution.py:74
  17.6 0.0 copy-start.2
  17.6 0.0 copy-start.1
  17.6 0.0 copy-start.7
  17.6 11.4 %all-to-all-done = bf16[12,24,512]{2,1,0:T(8,128)(2,1)S(1)} async-done(((bf16[12,24,512]{2,1,0:T(8,128)(2,1)}), bf16[12,24,512]{2,1,0:T(8,128)(2,1)S(1)}, u32[]{:S(2)}, u32[]{:S(2)}) %all-to-all-start) | async-done | bytes 294944 | tf_op jit(solution)/shard_map/all_to_all | solution.py:124
  29.0 4.5 %all-to-all-start.1 = ((bf16[4,128,2048]{2,1,0:T(8,128)(2,1)}), bf16[4,128,2048]{2,1,0:T(8,128)(2,1)}, u32[]{:S(2)}, u32[]{:S(2)}) async-start(bf16[4,128,2048]{2,1,0:T(8,128)(2,1)} %shard_map.109), calls=%async_computation.1 | async-start | bytes 4194304 | tf_op jit(solution)/shard_map/all_to_all | solution.py:128
  33.4 0.0 copy-done.2
  33.5 2.3 %collective-permute-start = (bf16[576,128]{1,0:T(8,128)(2,1)S(1)}, bf16[576,128]{1,0:T(8,128)(2,1)S(1)}, u32[]{:S(2)}, u32[]{:S(2)}) collective-permute-start(bf16[576,128]{1,0:T(8,128)(2,1)S(1)} %bitcast.60), channel_id=1, source_target_pairs={{0,64},{64,0},{128,192},{192,128},{256,320},{320,256},{384,448},{4... | collective-permute-start | bytes 442376 | tf_op jit(solution)/shard_map/ppermute | solution.py:136
  35.8 1.0 collective-permute-done
  36.9 3.8 %collective-permute-start.1 = (bf16[576,256]{1,0:T(8,128)(2,1)S(1)}, bf16[576,256]{1,0:T(8,128)(2,1)S(1)}, u32[]{:S(2)}, u32[]{:S(2)}) collective-permute-start(bf16[576,256]{1,0:T(8,128)(2,1)S(1)} %pad_maximum_fusion), channel_id=1, source_target_pairs={{0,128},{64,192},{128,0},{192,64},{256,384},{320,448},{384,256},{4... | collective-permute-start | bytes 884744 | tf_op jit(solution)/shard_map/ppermute | solution.py:136
  40.7 0.0 copy-done.1
  40.7 0.0 copy-done.7
  40.7 7.0 %fusion.11 = (f32[128]{0:T(128)S(1)}, f32[576,128]{1,0:T(8,128)}) fusion(bf16[1,128,576]{1,2,0:T(8,128)(2,1)S(1)} %copy-done.7, bf16[576,8192]{1,0:T(8,128)(2,1)} %param.16, bf16[1,128,8192]{2,1,0:T(8,128)(2,1)S(1)} %copy-done.1), kind=kOutput, calls=%fused_computation.15 | convolution fusion | flops 1208180608 | bytes 11977216 | tf_op jit(solution)/shard_map/dot_general | solution.py:131
  47.7 17.7 %collective-permute-done.1 = bf16[576,256]{1,0:T(8,128)(2,1)S(1)} collective-permute-done((bf16[576,256]{1,0:T(8,128)(2,1)S(1)}, bf16[576,256]{1,0:T(8,128)(2,1)S(1)}, u32[]{:S(2)}, u32[]{:S(2)}) %collective-permute-start.1) | collective-permute-done | bytes 294944 | tf_op jit(solution)/shard_map/ppermute | solution.py:136
  65.4 4.7 %collective-permute-start.2 = (bf16[288,512]{1,0:T(8,128)(2,1)S(1)}, bf16[288,512]{1,0:T(8,128)(2,1)S(1)}, u32[]{:S(2)}, u32[]{:S(2)}) collective-permute-start(bf16[288,512]{1,0:T(8,128)(2,1)S(1)} %bitcast.48), channel_id=1, source_target_pairs={{0,1},{1,2},{2,3},{3,4},{4,5},{5,6},{6,7},{7,0},{8,9},{9,10},{10,1... | collective-permute-start | bytes 884744 | tf_op jit(solution)/shard_map/ppermute | solution.py:96
  70.1 1.9 %collective-permute-start.3 = (bf16[288,512]{1,0:T(8,128)(2,1)S(1)}, bf16[288,512]{1,0:T(8,128)(2,1)S(1)}, u32[]{:S(2)}, u32[]{:S(2)}) collective-permute-start(bf16[288,512]{1,0:T(8,128)(2,1)S(1)} %bitcast.49), channel_id=1, source_target_pairs={{0,7},{1,0},{2,1},{3,2},{4,3},{5,4},{6,5},{7,6},{8,15},{9,8},{10,9... | collective-permute-start | bytes 884744 | tf_op jit(solution)/shard_map/ppermute | solution.py:96
  72.0 4.0 %collective-permute-done.2.refs_1_ = bf16[288,512]{1,0:T(8,128)(2,1)S(1)} collective-permute-done((bf16[288,512]{1,0:T(8,128)(2,1)S(1)}, bf16[288,512]{1,0:T(8,128)(2,1)S(1)}, u32[]{:S(2)}, u32[]{:S(2)}) %collective-permute-start.2) | collective-permute-done | bytes 294944 | tf_op jit(solution)/shard_map/ppermute | solution.py:96
  76.0 5.6 %collective-permute-start.4 = (bf16[288,512]{1,0:T(8,128)(2,1)S(1)}, bf16[288,512]{1,0:T(8,128)(2,1)S(1)}, u32[]{:S(2)}, u32[]{:S(2)}) collective-permute-start(bf16[288,512]{1,0:T(8,128)(2,1)S(1)} %collective-permute-done.2.refs_1_), channel_id=1, source_target_pairs={{0,1},{1,2},{2,3},{3,4},{4,5},{5,6},{6,7},{7,0},{8,9},{9,10},{10,1... | collective-permute-start | bytes 884744 | tf_op jit(solution)/shard_map/ppermute | solution.py:96
  81.7 0.0 collective-permute-done.3.refs_2_
  81.7 1.9 %collective-permute-start.5 = (bf16[288,512]{1,0:T(8,128)(2,1)S(1)}, bf16[288,512]{1,0:T(8,128)(2,1)S(1)}, u32[]{:S(2)}, u32[]{:S(2)}) collective-permute-start(bf16[288,512]{1,0:T(8,128)(2,1)S(1)} %collective-permute-done.3.refs_2_), channel_id=1, source_target_pairs={{0,7},{1,0},{2,1},{3,2},{4,3},{5,4},{6,5},{7,6},{8,15},{9,8},{10,9... | collective-permute-start | bytes 884744 | tf_op jit(solution)/shard_map/ppermute | solution.py:96
  83.6 3.1 %collective-permute-done.4.refs_3_ = bf16[288,512]{1,0:T(8,128)(2,1)S(1)} collective-permute-done((bf16[288,512]{1,0:T(8,128)(2,1)S(1)}, bf16[288,512]{1,0:T(8,128)(2,1)S(1)}, u32[]{:S(2)}, u32[]{:S(2)}) %collective-permute-start.4) | collective-permute-done | bytes 294944 | tf_op jit(solution)/shard_map/ppermute | solution.py:96
  86.7 5.6 %collective-permute-start.6 = (bf16[288,512]{1,0:T(8,128)(2,1)S(1)}, bf16[288,512]{1,0:T(8,128)(2,1)S(1)}, u32[]{:S(2)}, u32[]{:S(2)}) collective-permute-start(bf16[288,512]{1,0:T(8,128)(2,1)S(1)} %collective-permute-done.4.refs_3_), channel_id=1, source_target_pairs={{0,1},{1,2},{2,3},{3,4},{4,5},{5,6},{6,7},{7,0},{8,9},{9,10},{10,1... | collective-permute-start | bytes 884744 | tf_op jit(solution)/shard_map/ppermute | solution.py:96
  92.3 1.9 %collective-permute-start.10 = (f32[576,128]{1,0:T(8,128)}, f32[576,128]{1,0:T(8,128)S(1)}, u32[]{:S(2)}, u32[]{:S(2)}) collective-permute-start(f32[576,128]{1,0:T(8,128)} %get-tuple-element.22), channel_id=1, source_target_pairs={{0,7},{1,0},{2,1},{3,2},{4,3},{5,4},{6,5},{7,6},{8,15},{9,8},{10,9... | collective-permute-start | bytes 884744 | tf_op jit(solution)/shard_map/ppermute | solution.py:96
  94.3 0.1 broadcast_select_fusion.1
  94.4 0.0 collective-permute-done.5.refs_4_
  94.4 1.9 %collective-permute-start.7 = (bf16[288,512]{1,0:T(8,128)(2,1)S(1)}, bf16[288,512]{1,0:T(8,128)(2,1)S(1)}, u32[]{:S(2)}, u32[]{:S(2)}) collective-permute-start(bf16[288,512]{1,0:T(8,128)(2,1)S(1)} %collective-permute-done.5.refs_4_), channel_id=1, source_target_pairs={{0,7},{1,0},{2,1},{3,2},{4,3},{5,4},{6,5},{7,6},{8,15},{9,8},{10,9... | collective-permute-start | bytes 884744 | tf_op jit(solution)/shard_map/ppermute | solution.py:96
  96.3 0.2 collective-permute-done.6.refs_5_
  96.6 5.6 %collective-permute-start.8 = (bf16[288,512]{1,0:T(8,128)(2,1)S(1)}, bf16[288,512]{1,0:T(8,128)(2,1)S(1)}, u32[]{:S(2)}, u32[]{:S(2)}) collective-permute-start(bf16[288,512]{1,0:T(8,128)(2,1)S(1)} %collective-permute-done.6.refs_5_), channel_id=1, source_target_pairs={{0,1},{1,2},{2,3},{3,4},{4,5},{5,6},{6,7},{7,0},{8,9},{9,10},{10,1... | collective-permute-start | bytes 884744 | tf_op jit(solution)/shard_map/ppermute | solution.py:96
  102.2 3.6 %fusion.1 = bf16[2304,512]{1,0:T(8,128)(2,1)} fusion(s32[2304]{0:T(1024)S(1)} %fusion.18, bf16[576,256]{1,0:T(8,128)(2,1)S(1)} %get-tuple-element.24, bf16[576,256]{1,0:T(8,128)(2,1)S(1)} %get-tuple-element.23), kind=kOutput, calls=%fused_computation.2 | convolution fusion | flops 1362640896 | bytes 2958336 | tf_op jit(solution)/shard_map/dot_general | solution.py:150
  105.7 0.1 broadcast_select_fusion.4
  105.8 0.6 collective-permute-done.8.refs_0_
  106.4 0.0 all-to-all-done.1
  106.4 0.1 broadcast_in_dim.72.refs_14_.refs_2_
  106.5 2.4 %shard_map.111 = f32[1,512]{1,0:T(1,128)S(1)} custom-call(bf16[288,512]{1,0:T(8,128)(2,1)S(1)} %collective-permute-done.8.refs_0_, bf16[8,288,512]{2,1,0:T(8,128)(2,1)} %bitcast.51, bf16[4,48,512]{2,1,0:T(8,128)(2,1)S(1)} %broadcast_in_dim.72.refs_14_.refs_2_, bf16[512,2048]{1,0:T(8,128)(2,1)} %bitcast.11.refs_15_.refs_3_), custom_call_target="tpu_custom_call" | custom-call | flops 603979776 | bytes 2392064 | tf_op jit(solution)/shard_map/pallas_call | solution.py:54
  108.9 0.0 copy-start.3
  108.9 0.0 copy-start.4
  108.9 0.0 copy-start.9
  108.9 0.0 copy-start.8
  108.9 0.0 copy-start.5
  108.9 0.0 copy-start.6
  109.0 0.0 collective-permute-done.7.refs_6_
  109.0 6.7 %shard_map.110 = f32[1,512]{1,0:T(1,128)S(1)} custom-call(bf16[288,512]{1,0:T(8,128)(2,1)S(1)} %bitcast.50, bf16[288,512]{1,0:T(8,128)(2,1)S(1)} %collective-permute-done.2.refs_1_, bf16[288,512]{1,0:T(8,128)(2,1)S(1)} %collective-permute-done.3.refs_2_, bf16[288,512]{1,0:T(8,128)(2,1)S(1)} %collective-permute-done.4.refs_3_, ...), custom_call_target="tpu_custom_call" | custom-call | flops 4227858432 | bytes 4161536 | tf_op jit(solution)/shard_map/pallas_call | solution.py:54
  115.7 0.6 broadcast_in_dim.76
  116.3 0.0 copy-done.3
  116.3 0.0 copy-done.4
  116.3 0.7 select_reduce_fusion
  118.8 0.0 copy-done.9
  118.8 0.2 fusion.29
  119.0 13.0 %all-to-all-start.2 = ((f32[32,2,128]{2,1,0:T(2,128)}), f32[32,2,128]{2,1,0:T(2,128)S(1)}, u32[]{:S(2)}, u32[]{:S(2)}) async-start(f32[32,2,128]{2,1,0:T(2,128)} %bitcast.13), calls=%async_computation.2 | async-start | bytes 65536 | tf_op jit(solution)/shard_map/all_to_all | solution.py:177
  132.0 0.0 copy-done.8
  132.0 0.8 fusion.9
  132.8 11.4 %all-to-all-done.2 = f32[32,2,128]{2,1,0:T(2,128)S(1)} async-done(((f32[32,2,128]{2,1,0:T(2,128)}), f32[32,2,128]{2,1,0:T(2,128)S(1)}, u32[]{:S(2)}, u32[]{:S(2)}) %all-to-all-start.2) | async-done | bytes 32800 | tf_op jit(solution)/shard_map/all_to_all | solution.py:177
  144.3 0.0 copy-done.5
  144.3 0.0 copy-done.6
  144.3 1.2 fusion.33
  145.5 1.9 %collective-permute-start.9 = (f32[1,128]{1,0:T(1,128)S(1)}, f32[1,128]{1,0:T(1,128)S(1)}, u32[]{:S(2)}, u32[]{:S(2)}) collective-permute-start(f32[1,128]{1,0:T(1,128)S(1)} %fusion.33), channel_id=1, source_target_pairs={{0,7},{1,0},{2,1},{3,2},{4,3},{5,4},{6,5},{7,6},{8,15},{9,8},{10,9... | collective-permute-start | bytes 1544 | tf_op jit(solution)/shard_map/ppermute | solution.py:96
  147.4 0.0 collective-permute-done.10
  147.4 5.2 %collective-permute-done.9 = f32[1,128]{1,0:T(1,128)S(1)} collective-permute-done((f32[1,128]{1,0:T(1,128)S(1)}, f32[1,128]{1,0:T(1,128)S(1)}, u32[]{:S(2)}, u32[]{:S(2)}) %collective-permute-start.9) | collective-permute-done | bytes 544 | tf_op jit(solution)/shard_map/ppermute | solution.py:96
  152.6 0.7 fusion.12
  (12 shorter events, 0.2 us)
Async XLA Ops:
  1.9 27.1 %all-to-all-start = ((bf16[12,24,512]{2,1,0:T(8,128)(2,1)}), bf16[12,24,512]{2,1,0:T(8,128)(2,1)S(1)}, u32[]{:S(2)}, u32[]{:S(2)}) async-start(bf16[12,24,512]{2,1,0:T(8,128)(2,1)} %bitcast.2), calls=%async_computation | async-start | bytes 589824 | tf_op jit(solution)/shard_map/all_to_all | solution.py:124
  14.0 1.6 %copy-start = (bf16[1,128,8192]{2,1,0:T(8,128)(2,1)S(1)}, bf16[1,128,8192]{2,1,0:T(8,128)(2,1)}, u32[]{:S(2)}) copy-start(bf16[1,128,8192]{2,1,0:T(8,128)(2,1)} %param.13) | copy-start | bytes 6291460
  17.6 15.9 %copy-start.2 = (bf16[1,128,576]{1,2,0:T(8,128)(2,1)S(1)}, bf16[1,128,576]{1,2,0:T(8,128)(2,1)}, u32[]{:S(2)}) copy-start(bf16[1,128,576]{1,2,0:T(8,128)(2,1)} %param.12) | copy-start | bytes 442372
  17.6 23.1 %copy-start.1 = (bf16[1,128,8192]{2,1,0:T(8,128)(2,1)S(1)}, bf16[1,128,8192]{2,1,0:T(8,128)(2,1)}, u32[]{:S(2)}) copy-start(bf16[1,128,8192]{2,1,0:T(8,128)(2,1)} %param.13) | copy-start | bytes 6291460
  17.6 23.1 %copy-start.7 = (bf16[1,128,576]{1,2,0:T(8,128)(2,1)S(1)}, bf16[1,128,576]{1,2,0:T(8,128)(2,1)}, u32[]{:S(2)}) copy-start(bf16[1,128,576]{1,2,0:T(8,128)(2,1)} %param.11) | copy-start | bytes 442372
  29.0 77.4 %all-to-all-start.1 = ((bf16[4,128,2048]{2,1,0:T(8,128)(2,1)}), bf16[4,128,2048]{2,1,0:T(8,128)(2,1)}, u32[]{:S(2)}, u32[]{:S(2)}) async-start(bf16[4,128,2048]{2,1,0:T(8,128)(2,1)} %shard_map.109), calls=%async_computation.1 | async-start | bytes 4194304 | tf_op jit(solution)/shard_map/all_to_all | solution.py:128
  33.5 3.3 %collective-permute-start = (bf16[576,128]{1,0:T(8,128)(2,1)S(1)}, bf16[576,128]{1,0:T(8,128)(2,1)S(1)}, u32[]{:S(2)}, u32[]{:S(2)}) collective-permute-start(bf16[576,128]{1,0:T(8,128)(2,1)S(1)} %bitcast.60), channel_id=1, source_target_pairs={{0,64},{64,0},{128,192},{192,128},{256,320},{320,256},{384,448},{4... | collective-permute-start | bytes 442376 | tf_op jit(solution)/shard_map/ppermute | solution.py:136
  36.9 28.5 %collective-permute-start.1 = (bf16[576,256]{1,0:T(8,128)(2,1)S(1)}, bf16[576,256]{1,0:T(8,128)(2,1)S(1)}, u32[]{:S(2)}, u32[]{:S(2)}) collective-permute-start(bf16[576,256]{1,0:T(8,128)(2,1)S(1)} %pad_maximum_fusion), channel_id=1, source_target_pairs={{0,128},{64,192},{128,0},{192,64},{256,384},{320,448},{384,256},{4... | collective-permute-start | bytes 884744 | tf_op jit(solution)/shard_map/ppermute | solution.py:136
  65.4 10.6 %collective-permute-start.2 = (bf16[288,512]{1,0:T(8,128)(2,1)S(1)}, bf16[288,512]{1,0:T(8,128)(2,1)S(1)}, u32[]{:S(2)}, u32[]{:S(2)}) collective-permute-start(bf16[288,512]{1,0:T(8,128)(2,1)S(1)} %bitcast.48), channel_id=1, source_target_pairs={{0,1},{1,2},{2,3},{3,4},{4,5},{5,6},{6,7},{7,0},{8,9},{9,10},{10,1... | collective-permute-start | bytes 884744 | tf_op jit(solution)/shard_map/ppermute | solution.py:96
  70.1 11.5 %collective-permute-start.3 = (bf16[288,512]{1,0:T(8,128)(2,1)S(1)}, bf16[288,512]{1,0:T(8,128)(2,1)S(1)}, u32[]{:S(2)}, u32[]{:S(2)}) collective-permute-start(bf16[288,512]{1,0:T(8,128)(2,1)S(1)} %bitcast.49), channel_id=1, source_target_pairs={{0,7},{1,0},{2,1},{3,2},{4,3},{5,4},{6,5},{7,6},{8,15},{9,8},{10,9... | collective-permute-start | bytes 884744 | tf_op jit(solution)/shard_map/ppermute | solution.py:96
  76.0 10.7 %collective-permute-start.4 = (bf16[288,512]{1,0:T(8,128)(2,1)S(1)}, bf16[288,512]{1,0:T(8,128)(2,1)S(1)}, u32[]{:S(2)}, u32[]{:S(2)}) collective-permute-start(bf16[288,512]{1,0:T(8,128)(2,1)S(1)} %collective-permute-done.2.refs_1_), channel_id=1, source_target_pairs={{0,1},{1,2},{2,3},{3,4},{4,5},{5,6},{6,7},{7,0},{8,9},{9,10},{10,1... | collective-permute-start | bytes 884744 | tf_op jit(solution)/shard_map/ppermute | solution.py:96
  81.7 12.7 %collective-permute-start.5 = (bf16[288,512]{1,0:T(8,128)(2,1)S(1)}, bf16[288,512]{1,0:T(8,128)(2,1)S(1)}, u32[]{:S(2)}, u32[]{:S(2)}) collective-permute-start(bf16[288,512]{1,0:T(8,128)(2,1)S(1)} %collective-permute-done.3.refs_2_), channel_id=1, source_target_pairs={{0,7},{1,0},{2,1},{3,2},{4,3},{5,4},{6,5},{7,6},{8,15},{9,8},{10,9... | collective-permute-start | bytes 884744 | tf_op jit(solution)/shard_map/ppermute | solution.py:96
  86.7 9.8 %collective-permute-start.6 = (bf16[288,512]{1,0:T(8,128)(2,1)S(1)}, bf16[288,512]{1,0:T(8,128)(2,1)S(1)}, u32[]{:S(2)}, u32[]{:S(2)}) collective-permute-start(bf16[288,512]{1,0:T(8,128)(2,1)S(1)} %collective-permute-done.4.refs_3_), channel_id=1, source_target_pairs={{0,1},{1,2},{2,3},{3,4},{4,5},{5,6},{6,7},{7,0},{8,9},{9,10},{10,1... | collective-permute-start | bytes 884744 | tf_op jit(solution)/shard_map/ppermute | solution.py:96
  92.3 55.1 %collective-permute-start.10 = (f32[576,128]{1,0:T(8,128)}, f32[576,128]{1,0:T(8,128)S(1)}, u32[]{:S(2)}, u32[]{:S(2)}) collective-permute-start(f32[576,128]{1,0:T(8,128)} %get-tuple-element.22), channel_id=1, source_target_pairs={{0,7},{1,0},{2,1},{3,2},{4,3},{5,4},{6,5},{7,6},{8,15},{9,8},{10,9... | collective-permute-start | bytes 884744 | tf_op jit(solution)/shard_map/ppermute | solution.py:96
  94.4 14.5 %collective-permute-start.7 = (bf16[288,512]{1,0:T(8,128)(2,1)S(1)}, bf16[288,512]{1,0:T(8,128)(2,1)S(1)}, u32[]{:S(2)}, u32[]{:S(2)}) collective-permute-start(bf16[288,512]{1,0:T(8,128)(2,1)S(1)} %collective-permute-done.5.refs_4_), channel_id=1, source_target_pairs={{0,7},{1,0},{2,1},{3,2},{4,3},{5,4},{6,5},{7,6},{8,15},{9,8},{10,9... | collective-permute-start | bytes 884744 | tf_op jit(solution)/shard_map/ppermute | solution.py:96
  96.6 9.8 %collective-permute-start.8 = (bf16[288,512]{1,0:T(8,128)(2,1)S(1)}, bf16[288,512]{1,0:T(8,128)(2,1)S(1)}, u32[]{:S(2)}, u32[]{:S(2)}) collective-permute-start(bf16[288,512]{1,0:T(8,128)(2,1)S(1)} %collective-permute-done.6.refs_5_), channel_id=1, source_target_pairs={{0,1},{1,2},{2,3},{3,4},{4,5},{5,6},{6,7},{7,0},{8,9},{9,10},{10,1... | collective-permute-start | bytes 884744 | tf_op jit(solution)/shard_map/ppermute | solution.py:96
  108.9 7.4 %copy-start.3 = (s32[12]{0:T(128)S(1)}, s32[12]{0:T(128)}, u32[]{:S(2)}) copy-start(s32[12]{0:T(128)} %param.21) | copy-start | bytes 148
  108.9 7.4 %copy-start.4 = (s32[12]{0:T(128)S(1)}, s32[12]{0:T(128)}, u32[]{:S(2)}) copy-start(s32[12]{0:T(128)} %param.20) | copy-start | bytes 148
  108.9 9.9 %copy-start.9 = (s32[12]{0:T(128)S(1)}, s32[12]{0:T(128)}, u32[]{:S(2)}) copy-start(s32[12]{0:T(128)} %param.19) | copy-start | bytes 148
  108.9 23.1 %copy-start.8 = (f32[12]{0:T(128)S(1)}, f32[12]{0:T(128)}, u32[]{:S(2)}) copy-start(f32[12]{0:T(128)} %param.18) | copy-start | bytes 148
  108.9 35.4 %copy-start.5 = (f32[1,128]{1,0:T(1,128)S(1)}, f32[1,128]{1,0:T(1,128)}, u32[]{:S(2)}) copy-start(f32[1,128]{1,0:T(1,128)} %param.14) | copy-start | bytes 1540
  108.9 35.3 %copy-start.6 = (f32[1,128]{1,0:T(1,128)S(1)}, f32[1,128]{1,0:T(1,128)}, u32[]{:S(2)}) copy-start(f32[1,128]{1,0:T(1,128)} %param.15) | copy-start | bytes 1540
  119.0 25.3 %all-to-all-start.2 = ((f32[32,2,128]{2,1,0:T(2,128)}), f32[32,2,128]{2,1,0:T(2,128)S(1)}, u32[]{:S(2)}, u32[]{:S(2)}) async-start(f32[32,2,128]{2,1,0:T(2,128)} %bitcast.13), calls=%async_computation.2 | async-start | bytes 65536 | tf_op jit(solution)/shard_map/all_to_all | solution.py:177
  145.5 7.1 %collective-permute-start.9 = (f32[1,128]{1,0:T(1,128)S(1)}, f32[1,128]{1,0:T(1,128)S(1)}, u32[]{:S(2)}, u32[]{:S(2)}) collective-permute-start(f32[1,128]{1,0:T(1,128)S(1)} %fusion.33), channel_id=1, source_target_pairs={{0,7},{1,0},{2,1},{3,2},{4,3},{5,4},{6,5},{7,6},{8,15},{9,8},{10,9... | collective-permute-start | bytes 1544 | tf_op jit(solution)/shard_map/ppermute | solution.py:96

commit v2 on v1

--- a/solution.py
+++ b/solution.py
@@ -134,10 +134,6 @@
         feats = attn_frozen[0].T
         for bit in (1, 2):
             theirs = lax.ppermute(feats, "dp", [(d, d ^ bit) for d in range(n_dp)])
-            if bit == 2:
-                block, view_policy, part_policy, theirs = lax.optimization_barrier(
-                    (block, view_policy, part_policy, theirs)
-                )
             second = (member & bit) != 0
             feats = jnp.concatenate(
                 [jnp.where(second, theirs, feats), jnp.where(second, feats, theirs)], axis=1
@@ -153,8 +149,24 @@
         sub_mask = (sub_of_row[None, :] == jnp.arange(SUB, dtype=jnp.int32)[:, None]).astype(jnp.bfloat16)
         sub_mask = jnp.broadcast_to(sub_mask[:, :, None], (SUB, MASK_ROWS, shared))
 
+        block, view_policy, part_policy = lax.optimization_barrier((block, view_policy, part_policy))
+
         def sums(items):
             return block_sums(items, feats, seen, sub_mask)
+
+        def statistics(rewards, group_ids, prompt_len, response_len):
+            same_group = (group_ids[:, None] == group_ids[None, :]).astype(jnp.float32)
+            group_mean = jnp.dot(same_group, rewards, precision=lax.Precision.HIGHEST) / jnp.sum(same_group, axis=1)
+            advantage = rewards - group_mean
+            chosen = jnp.arange(rewards.shape[0], dtype=jnp.int32) == lax.axis_index("dp")
+            adv_one = jnp.sum(jnp.where(chosen, advantage, 0.0))
+            start_one = jnp.sum(jnp.where(chosen, prompt_len, 0))
+            length_one = jnp.sum(jnp.where(chosen, response_len, 0))
+            seq_total = tokens * n_pipe
+            positions = section * tokens + jnp.arange(tokens, dtype=jnp.int32)
+            inside = (positions >= start_one) & (positions < start_one + length_one)
+            weighting = jnp.where(inside, seq_total / length_one.astype(jnp.float32), 0.0)
+            return weighting, adv_one
 
         up, down = block, block
         arrived = [[(block, 0)]]
@@ -163,32 +175,19 @@
             down = shift(down, -1)
             arrived.append([(up, hop), (down, n_pipe - hop)])
         last = shift(up, 1)
-        total = sums(arrived[0] + arrived[1] + arrived[2] + arrived[3])
-        total += sums([(last, half)])
+        total = sums(arrived[0] + arrived[1] + arrived[2])
+        total += sums(arrived[3] + [(last, half)])
 
         frozen = total.reshape(MEMBERS, 1, tokens)
         me = jnp.arange(MEMBERS, dtype=jnp.int32)[:, None, None] == member
         policy = jnp.where(me, part_policy[None, None, :], 0.0)
         sent = jnp.concatenate([frozen, policy], axis=1)
         sent = jnp.broadcast_to(sent[:, None], (MEMBERS, n_tensor, 2, tokens)).reshape(MEMBERS * n_tensor, 2, tokens)
-        sent, rewards, group_ids, prompt_len, response_len = lax.optimization_barrier(
-            (sent, rewards, group_ids, prompt_len, response_len)
-        )
+        sent, *group = lax.optimization_barrier((sent, rewards, group_ids, prompt_len, response_len))
         gathered = lax.all_to_all(sent, ("dp", "tensor"), 0, 0, axis_index_groups=heads, tiled=True)
         summed = gathered.sum(axis=0)
 
-        same_group = (group_ids[:, None] == group_ids[None, :]).astype(jnp.float32)
-        group_mean = jnp.dot(same_group, rewards, precision=lax.Precision.HIGHEST) / jnp.sum(same_group, axis=1)
-        advantage = rewards - group_mean
-        chosen = jnp.arange(rewards.shape[0], dtype=jnp.int32) == lax.axis_index("dp")
-        adv_one = jnp.sum(jnp.where(chosen, advantage, 0.0))
-        start_one = jnp.sum(jnp.where(chosen, prompt_len, 0))
-        length_one = jnp.sum(jnp.where(chosen, response_len, 0))
-        seq_total = tokens * n_pipe
-        positions = section * tokens + jnp.arange(tokens, dtype=jnp.int32)
-        inside = (positions >= start_one) & (positions < start_one + length_one)
-        weighting = jnp.where(inside, seq_total / length_one.astype(jnp.float32), 0.0)
-
+        weighting, adv_one = statistics(*group)
         logp_frozen = rest_frozen[0] + summed[0]
         logp_policy = rest_policy[0] + summed[1]
         slope = weighting * (KL_WEIGHT * (1.0 - jnp.exp(logp_frozen - logp_policy)) - adv_one)

time: 154 us -> 133 us (0.86)
  waiting for transfers between devices: 54.6 us -> 36 us
  matrix products: 11.4 us -> 9.62 us
    ppermute x2, waiting for transfers between devices: 18.7 us -> 7.44 us  [shards(): theirs = lax.ppermute(feats, 'dp', [(d, d ^ bit) for d in range(n_dp)])]
    ppermute x9, waiting for transfers between devices: 13.1 us -> 8.42 us  [shift(): lax.ppermute(array, 'pipe', [(i, (i + by) % n_pipe) for i in range(n_pipe)])]
    all_to_all x1, waiting for transfers between devices: 11.4 us -> 8.71 us  [shards(): lax.all_to_all(sent, ('dp', 'tensor'), 0, 0, axis_index_groups=heads, til...]
    dot_general x1, matrix products: 7.01 us -> 5.19 us  [shards(): view_policy = jnp.dot(policy_out, own.T, preferred_element_type=jnp.float32)]
  transfers between devices with their start and end apart: 14 -> 14, of which waited for: 9 -> 6; matrix products, arithmetic and copies ran while one was open for 9% -> 10% of each run, Pallas kernels for 7% -> 8%
where the time goes in v2:
time: 133 us; the launch traced here: 132 us
  starting transfers between devices  65.6 us (49%)
  waiting for transfers between devices  36 us (27%)
  Pallas kernels  11.1 us (8%)
  matrix products  9.62 us (7%)
  local copies, waits for them, and re-layouts  4.21 us (3%)
  other arithmetic  3.1 us (2%)
  between operations  2.29 us (2%)
    ppermute x9, starting transfers between devices, shift(): lax.ppermute(array, 'pipe', [(i, (i + by) % n_pipe) for i in range(n_pipe)])  30.1 us
    all_to_all x1, starting transfers between devices, shards(): lax.all_to_all(sent, ('dp', 'tensor'), 0, 0, axis_index_groups=heads, til...  12.9 us
    all_to_all x1, starting transfers between devices, shards(): lax.all_to_all(parts.reshape(n_dp, unit_rows, step), 'dp', 0, 0, tiled=True)  12.1 us
    all_to_all x1, waiting for transfers between devices, shards(): lax.all_to_all(parts.reshape(n_dp, unit_rows, step), 'dp', 0, 0, tiled=True)  11.4 us
    pallas_call x2, Pallas kernels, block_sums(): pl.pallas_call(kernel, grid=(STEPS,), out_shape=jax.ShapeDtypeStruct((1,...  9.15 us
    all_to_all x1, waiting for transfers between devices, shards(): lax.all_to_all(sent, ('dp', 'tensor'), 0, 0, axis_index_groups=heads, til...  8.71 us
    ppermute x9, waiting for transfers between devices, shift(): lax.ppermute(array, 'pipe', [(i, (i + by) % n_pipe) for i in range(n_pipe)])  8.42 us
    ppermute x2, waiting for transfers between devices, shards(): theirs = lax.ppermute(feats, 'dp', [(d, d ^ bit) for d in range(n_dp)])  7.44 us
  transfers between devices with their start and end apart: 14, of which 6 were waited for; matrix products, arithmetic and copies ran while one was open for 10% of the time, Pallas kernels for 8%

profile of v2, /device:TPU:24, one launch (start us, length us, event | category | flops | bytes accessed | tf_op | source)
XLA Modules:
  0.0 131.9 jit_solution(15195860368875266917)
XLA Ops:
  0.0 1.1 reshape.190
  1.1 0.7 broadcast_in_dim.71
  1.9 12.1 %all-to-all-start = ((bf16[12,24,512]{2,1,0:T(8,128)(2,1)}), bf16[12,24,512]{2,1,0:T(8,128)(2,1)S(1)}, u32[]{:S(2)}, u32[]{:S(2)}) async-start(bf16[12,24,512]{2,1,0:T(8,128)(2,1)} %bitcast.2), calls=%async_computation | async-start | bytes 589824 | tf_op jit(solution)/shard_map/all_to_all | solution.py:124
  14.0 0.0 copy-start
  14.0 1.6 %copy-done = bf16[1,128,8192]{2,1,0:T(8,128)(2,1)S(1)} copy-done((bf16[1,128,8192]{2,1,0:T(8,128)(2,1)S(1)}, bf16[1,128,8192]{2,1,0:T(8,128)(2,1)}, u32[]{:S(2)}) %copy-start) | copy-done | bytes 2097176
  15.6 2.0 %shard_map.109 = bf16[4,128,2048]{2,1,0:T(8,128)(2,1)} custom-call(bf16[128,8192]{1,0:T(8,128)(2,1)S(1)} %bitcast.47), custom_call_target="tpu_custom_call" | custom-call | bytes 4194304 | tf_op jit(solution)/shard_map/pallas_call | solution.py:74
  17.6 0.0 copy-start.2
  17.6 0.0 copy-start.1
  17.6 0.0 copy-start.7
  17.6 11.4 %all-to-all-done = bf16[12,24,512]{2,1,0:T(8,128)(2,1)S(1)} async-done(((bf16[12,24,512]{2,1,0:T(8,128)(2,1)}), bf16[12,24,512]{2,1,0:T(8,128)(2,1)S(1)}, u32[]{:S(2)}, u32[]{:S(2)}) %all-to-all-start) | async-done | bytes 294944 | tf_op jit(solution)/shard_map/all_to_all | solution.py:124
  29.0 4.5 %all-to-all-start.1 = ((bf16[4,128,2048]{2,1,0:T(8,128)(2,1)}), bf16[4,128,2048]{2,1,0:T(8,128)(2,1)}, u32[]{:S(2)}, u32[]{:S(2)}) async-start(bf16[4,128,2048]{2,1,0:T(8,128)(2,1)} %shard_map.109), calls=%async_computation.1 | async-start | bytes 4194304 | tf_op jit(solution)/shard_map/all_to_all | solution.py:128
  33.4 0.0 copy-done.2
  33.5 2.3 %collective-permute-start.4 = (bf16[576,128]{1,0:T(8,128)(2,1)S(1)}, bf16[576,128]{1,0:T(8,128)(2,1)S(1)}, u32[]{:S(2)}, u32[]{:S(2)}) collective-permute-start(bf16[576,128]{1,0:T(8,128)(2,1)S(1)} %bitcast.60), channel_id=1, source_target_pairs={{0,64},{64,0},{128,192},{192,128},{256,320},{320,256},{384,448},{4... | collective-permute-start | bytes 442376 | tf_op jit(solution)/shard_map/ppermute | solution.py:136
  35.8 0.0 copy-done.1
  35.8 0.0 copy-done.7
  35.8 5.2 %fusion.11 = (f32[128]{0:T(128)S(1)}, f32[576,128]{1,0:T(8,128)S(1)}) fusion(bf16[1,128,576]{1,2,0:T(8,128)(2,1)S(1)} %copy-done.7, bf16[576,8192]{1,0:T(8,128)(2,1)} %param.16, bf16[1,128,8192]{2,1,0:T(8,128)(2,1)S(1)} %copy-done.1), kind=kOutput, calls=%fused_computation.15 | convolution fusion | flops 1208180608 | bytes 11977216 | tf_op jit(solution)/shard_map/dot_general | solution.py:131
  41.1 0.0 collective-permute-done.4
  41.2 4.7 %collective-permute-start = (bf16[288,512]{1,0:T(8,128)(2,1)S(1)}, bf16[288,512]{1,0:T(8,128)(2,1)S(1)}, u32[]{:S(2)}, u32[]{:S(2)}) collective-permute-start(bf16[288,512]{1,0:T(8,128)(2,1)S(1)} %bitcast.48), channel_id=1, source_target_pairs={{0,1},{1,2},{2,3},{3,4},{4,5},{5,6},{6,7},{7,0},{8,9},{9,10},{10,1... | collective-permute-start | bytes 884744 | tf_op jit(solution)/shard_map/ppermute | solution.py:96
  45.9 3.5 %collective-permute-start.5 = (bf16[576,256]{1,0:T(8,128)(2,1)S(1)}, bf16[576,256]{1,0:T(8,128)(2,1)S(1)}, u32[]{:S(2)}, u32[]{:S(2)}) collective-permute-start(bf16[576,256]{1,0:T(8,128)(2,1)S(1)} %pad_maximum_fusion), channel_id=1, source_target_pairs={{0,128},{64,192},{128,0},{192,64},{256,384},{320,448},{384,256},{4... | collective-permute-start | bytes 884744 | tf_op jit(solution)/shard_map/ppermute | solution.py:136
  49.5 1.9 %collective-permute-start.1 = (bf16[288,512]{1,0:T(8,128)(2,1)S(1)}, bf16[288,512]{1,0:T(8,128)(2,1)S(1)}, u32[]{:S(2)}, u32[]{:S(2)}) collective-permute-start(bf16[288,512]{1,0:T(8,128)(2,1)S(1)} %bitcast.49), channel_id=1, source_target_pairs={{0,7},{1,0},{2,1},{3,2},{4,3},{5,4},{6,5},{7,6},{8,15},{9,8},{10,9... | collective-permute-start | bytes 884744 | tf_op jit(solution)/shard_map/ppermute | solution.py:96
  51.4 0.9 collective-permute-done.refs_1_
  52.3 5.6 %collective-permute-start.2 = (bf16[288,512]{1,0:T(8,128)(2,1)S(1)}, bf16[288,512]{1,0:T(8,128)(2,1)S(1)}, u32[]{:S(2)}, u32[]{:S(2)}) collective-permute-start(bf16[288,512]{1,0:T(8,128)(2,1)S(1)} %collective-permute-done.refs_1_), channel_id=1, source_target_pairs={{0,1},{1,2},{2,3},{3,4},{4,5},{5,6},{6,7},{7,0},{8,9},{9,10},{10,1... | collective-permute-start | bytes 884744 | tf_op jit(solution)/shard_map/ppermute | solution.py:96
  58.0 7.4 %collective-permute-done.5 = bf16[576,256]{1,0:T(8,128)(2,1)S(1)} collective-permute-done((bf16[576,256]{1,0:T(8,128)(2,1)S(1)}, bf16[576,256]{1,0:T(8,128)(2,1)S(1)}, u32[]{:S(2)}, u32[]{:S(2)}) %collective-permute-start.5) | collective-permute-done | bytes 294944 | tf_op jit(solution)/shard_map/ppermute | solution.py:136
  65.4 0.1 broadcast_select_fusion.1
  65.5 0.0 collective-permute-done.1.refs_2_
  65.5 2.4 %collective-permute-start.3 = (bf16[288,512]{1,0:T(8,128)(2,1)S(1)}, bf16[288,512]{1,0:T(8,128)(2,1)S(1)}, u32[]{:S(2)}, u32[]{:S(2)}) collective-permute-start(bf16[288,512]{1,0:T(8,128)(2,1)S(1)} %collective-permute-done.1.refs_2_), channel_id=1, source_target_pairs={{0,7},{1,0},{2,1},{3,2},{4,3},{5,4},{6,5},{7,6},{8,15},{9,8},{10,9... | collective-permute-start | bytes 884744 | tf_op jit(solution)/shard_map/ppermute | solution.py:96
  67.9 0.0 collective-permute-done.2.refs_3_
  67.9 4.7 %collective-permute-start.6 = (bf16[288,512]{1,0:T(8,128)(2,1)S(1)}, bf16[288,512]{1,0:T(8,128)(2,1)S(1)}, u32[]{:S(2)}, u32[]{:S(2)}) collective-permute-start(bf16[288,512]{1,0:T(8,128)(2,1)S(1)} %collective-permute-done.2.refs_3_), channel_id=1, source_target_pairs={{0,1},{1,2},{2,3},{3,4},{4,5},{5,6},{6,7},{7,0},{8,9},{9,10},{10,1... | collective-permute-start | bytes 884744 | tf_op jit(solution)/shard_map/ppermute | solution.py:96
  72.6 3.6 %fusion.1 = bf16[2304,512]{1,0:T(8,128)(2,1)} fusion(s32[2304]{0:T(1024)S(1)} %fusion.18, bf16[576,256]{1,0:T(8,128)(2,1)S(1)} %get-tuple-element.22, bf16[576,256]{1,0:T(8,128)(2,1)S(1)} %get-tuple-element.21), kind=kOutput, calls=%fused_computation.2 | convolution fusion | flops 1362640896 | bytes 2958336 | tf_op jit(solution)/shard_map/dot_general | solution.py:146
  76.2 1.9 %collective-permute-start.10 = (f32[576,128]{1,0:T(8,128)S(1)}, f32[576,128]{1,0:T(8,128)S(1)}, u32[]{:S(2)}, u32[]{:S(2)}) collective-permute-start(f32[576,128]{1,0:T(8,128)S(1)} %get-tuple-element.20), channel_id=1, source_target_pairs={{0,7},{1,0},{2,1},{3,2},{4,3},{5,4},{6,5},{7,6},{8,15},{9,8},{10,9... | collective-permute-start | bytes 884744 | tf_op jit(solution)/shard_map/ppermute | solution.py:96
  78.1 0.0 collective-permute-done.3.refs_4_
  78.1 1.9 %collective-permute-start.7 = (bf16[288,512]{1,0:T(8,128)(2,1)S(1)}, bf16[288,512]{1,0:T(8,128)(2,1)S(1)}, u32[]{:S(2)}, u32[]{:S(2)}) collective-permute-start(bf16[288,512]{1,0:T(8,128)(2,1)S(1)} %collective-permute-done.3.refs_4_), channel_id=1, source_target_pairs={{0,7},{1,0},{2,1},{3,2},{4,3},{5,4},{6,5},{7,6},{8,15},{9,8},{10,9... | collective-permute-start | bytes 884744 | tf_op jit(solution)/shard_map/ppermute | solution.py:96
  80.1 0.0 collective-permute-done.6.refs_0_
  80.1 5.1 %collective-permute-start.8 = (bf16[288,512]{1,0:T(8,128)(2,1)S(1)}, bf16[288,512]{1,0:T(8,128)(2,1)S(1)}, u32[]{:S(2)}, u32[]{:S(2)}) collective-permute-start(bf16[288,512]{1,0:T(8,128)(2,1)S(1)} %collective-permute-done.6.refs_0_), channel_id=1, source_target_pairs={{0,1},{1,2},{2,3},{3,4},{4,5},{5,6},{6,7},{7,0},{8,9},{9,10},{10,1... | collective-permute-start | bytes 884744 | tf_op jit(solution)/shard_map/ppermute | solution.py:96
  85.2 0.1 broadcast_select_fusion.4
  85.3 0.0 all-to-all-done.1
  85.3 0.1 broadcast_in_dim.72.refs_10_.refs_6_
  85.4 5.3 %shard_map.110 = f32[1,512]{1,0:T(1,128)S(1)} custom-call(bf16[288,512]{1,0:T(8,128)(2,1)S(1)} %bitcast.50, bf16[288,512]{1,0:T(8,128)(2,1)S(1)} %collective-permute-done.refs_1_, bf16[288,512]{1,0:T(8,128)(2,1)S(1)} %collective-permute-done.1.refs_2_, bf16[288,512]{1,0:T(8,128)(2,1)S(1)} %collective-permute-done.2.refs_3_, ...), custom_call_target="tpu_custom_call" | custom-call | flops 3019898880 | bytes 3571712 | tf_op jit(solution)/shard_map/pallas_call | solution.py:54
  90.7 0.0 copy-start.9
  90.7 0.0 copy-start.3
  90.7 0.0 copy-start.4
  90.7 0.0 copy-start.8
  90.8 0.0 copy-start.5
  90.8 0.0 copy-start.6
  90.8 2.7 %collective-permute-done.7.refs_1_ = bf16[288,512]{1,0:T(8,128)(2,1)S(1)} collective-permute-done((bf16[288,512]{1,0:T(8,128)(2,1)S(1)}, bf16[288,512]{1,0:T(8,128)(2,1)S(1)}, u32[]{:S(2)}, u32[]{:S(2)}) %collective-permute-start.7) | collective-permute-done | bytes 294944 | tf_op jit(solution)/shard_map/ppermute | solution.py:96
  93.5 0.0 collective-permute-done.8.refs_2_
  93.5 3.8 %shard_map.111 = f32[1,512]{1,0:T(1,128)S(1)} custom-call(bf16[288,512]{1,0:T(8,128)(2,1)S(1)} %collective-permute-done.6.refs_0_, bf16[288,512]{1,0:T(8,128)(2,1)S(1)} %collective-permute-done.7.refs_1_, bf16[288,512]{1,0:T(8,128)(2,1)S(1)} %collective-permute-done.8.refs_2_, bf16[8,288,512]{2,1,0:T(8,128)(2,1)} %bitcast.56, bf16[8,288,512]{2,1,0:T(8,128)(2,1)} %bitcast.57, ...), custom_call_target="tpu_custom_call" | custom-call | flops 1811939328 | bytes 2981888 | tf_op jit(solution)/shard_map/pallas_call | solution.py:54
  97.4 0.6 broadcast_in_dim.76
  98.0 12.9 %all-to-all-start.2 = ((f32[32,2,128]{2,1,0:T(2,128)}), f32[32,2,128]{2,1,0:T(2,128)S(1)}, u32[]{:S(2)}, u32[]{:S(2)}) async-start(f32[32,2,128]{2,1,0:T(2,128)} %bitcast.13), calls=%async_computation.2 | async-start | bytes 65536 | tf_op jit(solution)/shard_map/all_to_all | solution.py:187
  111.0 0.0 copy-done.9
  111.0 0.2 fusion.29
  111.2 0.0 copy-done.3
  111.2 0.0 copy-done.4
  111.2 0.7 select_reduce_fusion
  113.7 0.0 copy-done.8
  113.7 0.8 fusion.9
  114.5 8.7 %all-to-all-done.2 = f32[32,2,128]{2,1,0:T(2,128)S(1)} async-done(((f32[32,2,128]{2,1,0:T(2,128)}), f32[32,2,128]{2,1,0:T(2,128)S(1)}, u32[]{:S(2)}, u32[]{:S(2)}) %all-to-all-start.2) | async-done | bytes 32800 | tf_op jit(solution)/shard_map/all_to_all | solution.py:187
  123.3 0.0 copy-done.5
  123.3 0.0 copy-done.6
  123.3 1.2 fusion.33
  124.5 1.9 %collective-permute-start.9 = (f32[1,128]{1,0:T(1,128)S(1)}, f32[1,128]{1,0:T(1,128)S(1)}, u32[]{:S(2)}, u32[]{:S(2)}) collective-permute-start(f32[1,128]{1,0:T(1,128)S(1)} %fusion.33), channel_id=1, source_target_pairs={{0,7},{1,0},{2,1},{3,2},{4,3},{5,4},{6,5},{7,6},{8,15},{9,8},{10,9... | collective-permute-start | bytes 1544 | tf_op jit(solution)/shard_map/ppermute | solution.py:96
  126.4 0.0 collective-permute-done.10
  126.5 4.7 %collective-permute-done.9 = f32[1,128]{1,0:T(1,128)S(1)} collective-permute-done((f32[1,128]{1,0:T(1,128)S(1)}, f32[1,128]{1,0:T(1,128)S(1)}, u32[]{:S(2)}, u32[]{:S(2)}) %collective-permute-start.9) | collective-permute-done | bytes 544 | tf_op jit(solution)/shard_map/ppermute | solution.py:96
  131.2 0.7 fusion.12
  (12 shorter events, 0.2 us)
Async XLA Ops:
  1.9 27.1 %all-to-all-start = ((bf16[12,24,512]{2,1,0:T(8,128)(2,1)}), bf16[12,24,512]{2,1,0:T(8,128)(2,1)S(1)}, u32[]{:S(2)}, u32[]{:S(2)}) async-start(bf16[12,24,512]{2,1,0:T(8,128)(2,1)} %bitcast.2), calls=%async_computation | async-start | bytes 589824 | tf_op jit(solution)/shard_map/all_to_all | solution.py:124
  14.0 1.6 %copy-start = (bf16[1,128,8192]{2,1,0:T(8,128)(2,1)S(1)}, bf16[1,128,8192]{2,1,0:T(8,128)(2,1)}, u32[]{:S(2)}) copy-start(bf16[1,128,8192]{2,1,0:T(8,128)(2,1)} %param.13) | copy-start | bytes 6291460
  17.6 15.9 %copy-start.2 = (bf16[1,128,576]{1,2,0:T(8,128)(2,1)S(1)}, bf16[1,128,576]{1,2,0:T(8,128)(2,1)}, u32[]{:S(2)}) copy-start(bf16[1,128,576]{1,2,0:T(8,128)(2,1)} %param.12) | copy-start | bytes 442372
  17.6 18.2 %copy-start.1 = (bf16[1,128,8192]{2,1,0:T(8,128)(2,1)S(1)}, bf16[1,128,8192]{2,1,0:T(8,128)(2,1)}, u32[]{:S(2)}) copy-start(bf16[1,128,8192]{2,1,0:T(8,128)(2,1)} %param.13) | copy-start | bytes 6291460
  17.6 18.3 %copy-start.7 = (bf16[1,128,576]{1,2,0:T(8,128)(2,1)S(1)}, bf16[1,128,576]{1,2,0:T(8,128)(2,1)}, u32[]{:S(2)}) copy-start(bf16[1,128,576]{1,2,0:T(8,128)(2,1)} %param.11) | copy-start | bytes 442372
  29.0 56.3 %all-to-all-start.1 = ((bf16[4,128,2048]{2,1,0:T(8,128)(2,1)}), bf16[4,128,2048]{2,1,0:T(8,128)(2,1)}, u32[]{:S(2)}, u32[]{:S(2)}) async-start(bf16[4,128,2048]{2,1,0:T(8,128)(2,1)} %shard_map.109), calls=%async_computation.1 | async-start | bytes 4194304 | tf_op jit(solution)/shard_map/all_to_all | solution.py:128
  33.5 7.6 %collective-permute-start.4 = (bf16[576,128]{1,0:T(8,128)(2,1)S(1)}, bf16[576,128]{1,0:T(8,128)(2,1)S(1)}, u32[]{:S(2)}, u32[]{:S(2)}) collective-permute-start(bf16[576,128]{1,0:T(8,128)(2,1)S(1)} %bitcast.60), channel_id=1, source_target_pairs={{0,64},{64,0},{128,192},{192,128},{256,320},{320,256},{384,448},{4... | collective-permute-start | bytes 442376 | tf_op jit(solution)/shard_map/ppermute | solution.py:136
  41.2 11.2 %collective-permute-start = (bf16[288,512]{1,0:T(8,128)(2,1)S(1)}, bf16[288,512]{1,0:T(8,128)(2,1)S(1)}, u32[]{:S(2)}, u32[]{:S(2)}) collective-permute-start(bf16[288,512]{1,0:T(8,128)(2,1)S(1)} %bitcast.48), channel_id=1, source_target_pairs={{0,1},{1,2},{2,3},{3,4},{4,5},{5,6},{6,7},{7,0},{8,9},{9,10},{10,1... | collective-permute-start | bytes 884744 | tf_op jit(solution)/shard_map/ppermute | solution.py:96
  45.9 19.5 %collective-permute-start.5 = (bf16[576,256]{1,0:T(8,128)(2,1)S(1)}, bf16[576,256]{1,0:T(8,128)(2,1)S(1)}, u32[]{:S(2)}, u32[]{:S(2)}) collective-permute-start(bf16[576,256]{1,0:T(8,128)(2,1)S(1)} %pad_maximum_fusion), channel_id=1, source_target_pairs={{0,128},{64,192},{128,0},{192,64},{256,384},{320,448},{384,256},{4... | collective-permute-start | bytes 884744 | tf_op jit(solution)/shard_map/ppermute | solution.py:136
  49.5 16.1 %collective-permute-start.1 = (bf16[288,512]{1,0:T(8,128)(2,1)S(1)}, bf16[288,512]{1,0:T(8,128)(2,1)S(1)}, u32[]{:S(2)}, u32[]{:S(2)}) collective-permute-start(bf16[288,512]{1,0:T(8,128)(2,1)S(1)} %bitcast.49), channel_id=1, source_target_pairs={{0,7},{1,0},{2,1},{3,2},{4,3},{5,4},{6,5},{7,6},{8,15},{9,8},{10,9... | collective-permute-start | bytes 884744 | tf_op jit(solution)/shard_map/ppermute | solution.py:96
  52.3 15.6 %collective-permute-start.2 = (bf16[288,512]{1,0:T(8,128)(2,1)S(1)}, bf16[288,512]{1,0:T(8,128)(2,1)S(1)}, u32[]{:S(2)}, u32[]{:S(2)}) collective-permute-start(bf16[288,512]{1,0:T(8,128)(2,1)S(1)} %collective-permute-done.refs_1_), channel_id=1, source_target_pairs={{0,1},{1,2},{2,3},{3,4},{4,5},{5,6},{6,7},{7,0},{8,9},{9,10},{10,1... | collective-permute-start | bytes 884744 | tf_op jit(solution)/shard_map/ppermute | solution.py:96
  65.5 12.6 %collective-permute-start.3 = (bf16[288,512]{1,0:T(8,128)(2,1)S(1)}, bf16[288,512]{1,0:T(8,128)(2,1)S(1)}, u32[]{:S(2)}, u32[]{:S(2)}) collective-permute-start(bf16[288,512]{1,0:T(8,128)(2,1)S(1)} %collective-permute-done.1.refs_2_), channel_id=1, source_target_pairs={{0,7},{1,0},{2,1},{3,2},{4,3},{5,4},{6,5},{7,6},{8,15},{9,8},{10,9... | collective-permute-start | bytes 884744 | tf_op jit(solution)/shard_map/ppermute | solution.py:96
  67.9 12.2 %collective-permute-start.6 = (bf16[288,512]{1,0:T(8,128)(2,1)S(1)}, bf16[288,512]{1,0:T(8,128)(2,1)S(1)}, u32[]{:S(2)}, u32[]{:S(2)}) collective-permute-start(bf16[288,512]{1,0:T(8,128)(2,1)S(1)} %collective-permute-done.2.refs_3_), channel_id=1, source_target_pairs={{0,1},{1,2},{2,3},{3,4},{4,5},{5,6},{6,7},{7,0},{8,9},{9,10},{10,1... | collective-permute-start | bytes 884744 | tf_op jit(solution)/shard_map/ppermute | solution.py:96
  76.2 50.2 %collective-permute-start.10 = (f32[576,128]{1,0:T(8,128)S(1)}, f32[576,128]{1,0:T(8,128)S(1)}, u32[]{:S(2)}, u32[]{:S(2)}) collective-permute-start(f32[576,128]{1,0:T(8,128)S(1)} %get-tuple-element.20), channel_id=1, source_target_pairs={{0,7},{1,0},{2,1},{3,2},{4,3},{5,4},{6,5},{7,6},{8,15},{9,8},{10,9... | collective-permute-start | bytes 884744 | tf_op jit(solution)/shard_map/ppermute | solution.py:96
  78.1 15.4 %collective-permute-start.7 = (bf16[288,512]{1,0:T(8,128)(2,1)S(1)}, bf16[288,512]{1,0:T(8,128)(2,1)S(1)}, u32[]{:S(2)}, u32[]{:S(2)}) collective-permute-start(bf16[288,512]{1,0:T(8,128)(2,1)S(1)} %collective-permute-done.3.refs_4_), channel_id=1, source_target_pairs={{0,7},{1,0},{2,1},{3,2},{4,3},{5,4},{6,5},{7,6},{8,15},{9,8},{10,9... | collective-permute-start | bytes 884744 | tf_op jit(solution)/shard_map/ppermute | solution.py:96
  80.1 13.4 %collective-permute-start.8 = (bf16[288,512]{1,0:T(8,128)(2,1)S(1)}, bf16[288,512]{1,0:T(8,128)(2,1)S(1)}, u32[]{:S(2)}, u32[]{:S(2)}) collective-permute-start(bf16[288,512]{1,0:T(8,128)(2,1)S(1)} %collective-permute-done.6.refs_0_), channel_id=1, source_target_pairs={{0,1},{1,2},{2,3},{3,4},{4,5},{5,6},{6,7},{7,0},{8,9},{9,10},{10,1... | collective-permute-start | bytes 884744 | tf_op jit(solution)/shard_map/ppermute | solution.py:96
  90.7 20.3 %copy-start.9 = (s32[12]{0:T(128)S(1)}, s32[12]{0:T(128)}, u32[]{:S(2)}) copy-start(s32[12]{0:T(128)} %param.19) | copy-start | bytes 148
  90.7 20.4 %copy-start.3 = (s32[12]{0:T(128)S(1)}, s32[12]{0:T(128)}, u32[]{:S(2)}) copy-start(s32[12]{0:T(128)} %param.21) | copy-start | bytes 148
  90.7 20.4 %copy-start.4 = (s32[12]{0:T(128)S(1)}, s32[12]{0:T(128)}, u32[]{:S(2)}) copy-start(s32[12]{0:T(128)} %param.20) | copy-start | bytes 148
  90.7 23.0 %copy-start.8 = (f32[12]{0:T(128)S(1)}, f32[12]{0:T(128)}, u32[]{:S(2)}) copy-start(f32[12]{0:T(128)} %param.18) | copy-start | bytes 148
  90.8 32.5 %copy-start.5 = (f32[1,128]{1,0:T(1,128)S(1)}, f32[1,128]{1,0:T(1,128)}, u32[]{:S(2)}) copy-start(f32[1,128]{1,0:T(1,128)} %param.14) | copy-start | bytes 1540
  90.8 32.5 %copy-start.6 = (f32[1,128]{1,0:T(1,128)S(1)}, f32[1,128]{1,0:T(1,128)}, u32[]{:S(2)}) copy-start(f32[1,128]{1,0:T(1,128)} %param.15) | copy-start | bytes 1540
  98.0 25.2 %all-to-all-start.2 = ((f32[32,2,128]{2,1,0:T(2,128)}), f32[32,2,128]{2,1,0:T(2,128)S(1)}, u32[]{:S(2)}, u32[]{:S(2)}) async-start(f32[32,2,128]{2,1,0:T(2,128)} %bitcast.13), calls=%async_computation.2 | async-start | bytes 65536 | tf_op jit(solution)/shard_map/all_to_all | solution.py:187
  124.5 6.7 %collective-permute-start.9 = (f32[1,128]{1,0:T(1,128)S(1)}, f32[1,128]{1,0:T(1,128)S(1)}, u32[]{:S(2)}, u32[]{:S(2)}) collective-permute-start(f32[1,128]{1,0:T(1,128)S(1)} %fusion.33), channel_id=1, source_target_pairs={{0,7},{1,0},{2,1},{3,2},{4,3},{5,4},{6,5},{7,6},{8,15},{9,8},{10,9... | collective-permute-start | bytes 1544 | tf_op jit(solution)/shard_map/ppermute | solution.py:96

commit v3 on v2

--- a/solution.py
+++ b/solution.py
@@ -9,31 +9,32 @@
 AXES = ("dp", "tensor", "pipe")
 MEMBERS = 4
 SUB = 4
-MASK_ROWS = 48
 STEPS = 2
 VMEM_BYTES = 24 * 1024 * 1024
 
 
-def block_sums(items, feats, seen, sub_mask):
+def block_sums(items, feats, seen):
     count = len(items)
     tokens = seen.shape[0]
     step = items[0][0].shape[1]
+    n = feats.shape[1]
 
     def kernel(*refs):
-        mask_ref, seen_ref, out_ref = refs[2 * count :]
+        seen_ref, out_ref = refs[2 * count :]
+        first = pl.program_id(0) * (SUB // STEPS)
+        view = jnp.zeros((count * n, tokens), jnp.float32)
+        for k in range(SUB // STEPS):
+            part = pl.ds(pl.multiple_of((first + k) * n, 8), n)
+            view += lax.dot_general(
+                jnp.concatenate([r[part, :] for r in refs[:count]], axis=0),
+                seen_ref[:, k * step : (k + 1) * step],
+                (((1,), (1,)), ((), ())),
+                preferred_element_type=jnp.float32,
+            )
         total = jnp.zeros((1, tokens), jnp.float32)
-        for k in range(SUB // STEPS):
-            terms = jnp.zeros((MASK_ROWS, tokens), jnp.float32)
-            for row_ref, feat_ref in zip(refs[:count], refs[count : 2 * count]):
-                view = lax.dot_general(
-                    row_ref[...],
-                    seen_ref[:, k * step : (k + 1) * step],
-                    (((1,), (1,)), ((), ())),
-                    preferred_element_type=jnp.float32,
-                )
-                for at in range(0, row_ref.shape[0], MASK_ROWS):
-                    terms += view[at : at + MASK_ROWS] * feat_ref[0, at : at + MASK_ROWS, :].astype(jnp.float32)
-            total += jnp.sum(terms * mask_ref[k].astype(jnp.float32), axis=0, keepdims=True)
+        for i, feat_ref in enumerate(refs[count : 2 * count]):
+            terms = view[i * n : (i + 1) * n] * feat_ref[0].astype(jnp.float32)
+            total += jnp.sum(terms, axis=0, keepdims=True)
 
         @pl.when(pl.program_id(0) == 0)
         def _():
@@ -48,7 +49,6 @@
     specs = [pl.BlockSpec(x.shape, lambda k: (0, 0)) for x in blocks]
     specs += [pl.BlockSpec((1, *feats.shape[1:]), lambda k, at=at: (at, 0, 0)) for _, at in items]
     specs += [
-        pl.BlockSpec((SUB // STEPS, MASK_ROWS, tokens), lambda k: (k, 0, 0)),
         pl.BlockSpec((tokens, step * SUB // STEPS), lambda k: (0, k)),
     ]
     return pl.pallas_call(
@@ -61,7 +61,7 @@
             flops=2 * rows * SUB * step * tokens, bytes_accessed=rows * step * 2 + 2 * seen.size, transcendentals=0
         ),
         compiler_params=pltpu.CompilerParams(dimension_semantics=("arbitrary",), vmem_limit_bytes=VMEM_BYTES),
-    )(*blocks, *[feats] * count, sub_mask, seen)
+    )(*blocks, *[feats] * count, seen)
 
 
 def column_parts(array, count):
@@ -122,7 +122,11 @@
         parts = frozen_out.reshape(rows, MEMBERS, SUB, step).transpose(1, 2, 0, 3).reshape(MEMBERS, unit_rows, step)
         parts = jnp.broadcast_to(parts[None], (n_dp // MEMBERS, MEMBERS, unit_rows, step))
         block = lax.all_to_all(parts.reshape(n_dp, unit_rows, step), "dp", 0, 0, tiled=True)
-        block = block.reshape(block_rows, step)
+        at = jnp.arange(block_rows, dtype=jnp.int32)
+        source = at // rows % n_dp * unit_rows + at // (n_dp * rows) * rows + at % rows
+        order = (source[:, None] == at[None, :]).astype(jnp.bfloat16)
+        block = jnp.dot(order, block.reshape(block_rows, step), preferred_element_type=jnp.float32)
+        block = block.astype(jnp.bfloat16)
 
         split = column_parts(own, MEMBERS)
         seen = lax.all_to_all(split, "dp", 0, 0, axis_index_groups=groups, tiled=True).reshape(shared, quarter)
@@ -138,21 +142,18 @@
             feats = jnp.concatenate(
                 [jnp.where(second, theirs, feats), jnp.where(second, feats, theirs)], axis=1
             )
-        at = jnp.arange(n_pipe * block_rows, dtype=jnp.int32)
-        source = at // unit_rows % n_dp * n_pipe + (section - at // block_rows) % n_pipe
+        at = jnp.arange(n_pipe * n_dp * rows, dtype=jnp.int32)
+        source = at // rows % n_dp * n_pipe + (section - at // (n_dp * rows)) % n_pipe
         source = source * rows + at % rows
         columns = jnp.arange(n_dp * n_pipe * rows, dtype=jnp.int32)
         pick = (source[:, None] == columns[None, :]).astype(jnp.bfloat16)
         feats = jnp.dot(pick, feats, preferred_element_type=jnp.float32).astype(jnp.bfloat16)
-        feats = in_hbm(feats.reshape(n_pipe, block_rows, shared))
-        sub_of_row = jnp.arange(MASK_ROWS, dtype=jnp.int32) // rows % SUB
-        sub_mask = (sub_of_row[None, :] == jnp.arange(SUB, dtype=jnp.int32)[:, None]).astype(jnp.bfloat16)
-        sub_mask = jnp.broadcast_to(sub_mask[:, :, None], (SUB, MASK_ROWS, shared))
+        feats = in_hbm(feats.reshape(n_pipe, n_dp * rows, shared))
 
         block, view_policy, part_policy = lax.optimization_barrier((block, view_policy, part_policy))
 
         def sums(items):
-            return block_sums(items, feats, seen, sub_mask)
+            return block_sums(items, feats, seen)
 
         def statistics(rewards, group_ids, prompt_len, response_len):
             same_group = (group_ids[:, None] == group_ids[None, :]).astype(jnp.float32)
@@ -175,8 +176,8 @@
             down = shift(down, -1)
             arrived.append([(up, hop), (down, n_pipe - hop)])
         last = shift(up, 1)
-        total = sums(arrived[0] + arrived[1] + arrived[2])
-        total += sums(arrived[3] + [(last, half)])
+        total = sums(arrived[0] + arrived[1] + arrived[2] + arrived[3])
+        total += sums([(last, half)])
 
         frozen = total.reshape(MEMBERS, 1, tokens)
         me = jnp.arange(MEMBERS, dtype=jnp.int32)[:, None, None] == member

time: 133 us -> 129 us (0.970)
  the two profiles are of different devices: /device:TPU:24 before, /device:TPU:1 now
where the time goes in v3:
time: 129 us; the launch traced here: 128 us
  starting transfers between devices  70.5 us (55%)
  waiting for transfers between devices  33.3 us (26%)
  matrix products  7.89 us (6%)
  Pallas kernels  7.12 us (6%)
  local copies, waits for them, and re-layouts  4.12 us (3%)
  other arithmetic  3.1 us (2%)
  between operations  2.25 us (2%)
    ppermute x9, starting transfers between devices, shift(): lax.ppermute(array, 'pipe', [(i, (i + by) % n_pipe) for i in range(n_pipe)])  28.8 us
    all_to_all x1, starting transfers between devices, shards(): lax.all_to_all(sent, ('dp', 'tensor'), 0, 0, axis_index_groups=heads, til...  17.2 us
    all_to_all x1, starting transfers between devices, shards(): lax.all_to_all(parts.reshape(n_dp, unit_rows, step), 'dp', 0, 0, tiled=True)  13.9 us
    ppermute x9, waiting for transfers between devices, shift(): lax.ppermute(array, 'pipe', [(i, (i + by) % n_pipe) for i in range(n_pipe)])  11.3 us
    all_to_all x1, waiting for transfers between devices, shards(): lax.all_to_all(parts.reshape(n_dp, unit_rows, step), 'dp', 0, 0, tiled=True)  11.1 us
    all_to_all x1, waiting for transfers between devices, shards(): lax.all_to_all(sent, ('dp', 'tensor'), 0, 0, axis_index_groups=heads, til...  10.9 us
    ppermute x2, starting transfers between devices, shards(): theirs = lax.ppermute(feats, 'dp', [(d, d ^ bit) for d in range(n_dp)])  5.88 us
    dot_general x1, matrix products, shards(): view_policy = jnp.dot(policy_out, own.T, preferred_element_type=jnp.float32)  5.2 us
  transfers between devices with their start and end apart: 14, of which 7 were waited for; matrix products, arithmetic and copies ran while one was open for 9% of the time, Pallas kernels for 6%

profile of v3, /device:TPU:1, one launch (start us, length us, event | category | flops | bytes accessed | tf_op | source)
XLA Modules:
  0.0 128.3 jit_solution(5318129223115439474)
XLA Ops:
  0.0 1.1 reshape.178
  1.1 0.7 broadcast_in_dim.63
  1.9 13.9 %all-to-all-start = ((bf16[12,24,512]{2,1,0:T(8,128)(2,1)}), bf16[12,24,512]{2,1,0:T(8,128)(2,1)S(1)}, u32[]{:S(2)}, u32[]{:S(2)}) async-start(bf16[12,24,512]{2,1,0:T(8,128)(2,1)} %bitcast.2), calls=%async_computation | async-start | bytes 589824 | tf_op jit(solution)/shard_map/all_to_all | solution.py:124
  15.7 0.0 copy-start
  15.7 1.6 %copy-done = bf16[1,128,8192]{2,1,0:T(8,128)(2,1)S(1)} copy-done((bf16[1,128,8192]{2,1,0:T(8,128)(2,1)S(1)}, bf16[1,128,8192]{2,1,0:T(8,128)(2,1)}, u32[]{:S(2)}) %copy-start) | copy-done | bytes 2097176
  17.3 2.0 %shard_map.109 = bf16[4,128,2048]{2,1,0:T(8,128)(2,1)} custom-call(bf16[128,8192]{1,0:T(8,128)(2,1)S(1)} %bitcast.48), custom_call_target="tpu_custom_call" | custom-call | bytes 4194304 | tf_op jit(solution)/shard_map/pallas_call | solution.py:74
  19.3 0.0 copy-start.2
  19.3 0.0 copy-start.1
  19.3 0.0 copy-start.7
  19.3 11.1 %all-to-all-done = bf16[12,24,512]{2,1,0:T(8,128)(2,1)S(1)} async-done(((bf16[12,24,512]{2,1,0:T(8,128)(2,1)}), bf16[12,24,512]{2,1,0:T(8,128)(2,1)S(1)}, u32[]{:S(2)}, u32[]{:S(2)}) %all-to-all-start) | async-done | bytes 294944 | tf_op jit(solution)/shard_map/all_to_all | solution.py:124
  30.4 4.8 %all-to-all-start.1 = ((bf16[4,128,2048]{2,1,0:T(8,128)(2,1)}), bf16[4,128,2048]{2,1,0:T(8,128)(2,1)}, u32[]{:S(2)}, u32[]{:S(2)}) async-start(bf16[4,128,2048]{2,1,0:T(8,128)(2,1)} %shard_map.109), calls=%async_computation.1 | async-start | bytes 4194304 | tf_op jit(solution)/shard_map/all_to_all | solution.py:132
  35.2 0.0 copy-done.2
  35.2 2.0 %collective-permute-start.6 = (bf16[576,128]{1,0:T(8,128)(2,1)S(1)}, bf16[576,128]{1,0:T(8,128)(2,1)S(1)}, u32[]{:S(2)}, u32[]{:S(2)}) collective-permute-start(bf16[576,128]{1,0:T(8,128)(2,1)S(1)} %bitcast.59), channel_id=1, source_target_pairs={{0,64},{64,0},{128,192},{192,128},{256,320},{320,256},{384,448},{4... | collective-permute-start | bytes 442376 | tf_op jit(solution)/shard_map/ppermute | solution.py:140
  37.2 0.0 copy-done.1
  37.2 0.0 copy-done.7
  37.2 5.2 %fusion.11 = (f32[128]{0:T(128)S(1)}, f32[576,128]{1,0:T(8,128)S(1)}) fusion(bf16[1,128,576]{1,2,0:T(8,128)(2,1)S(1)} %copy-done.7, bf16[576,8192]{1,0:T(8,128)(2,1)} %param.16, bf16[1,128,8192]{2,1,0:T(8,128)(2,1)S(1)} %copy-done.1), kind=kOutput, calls=%fused_computation.17 | convolution fusion | flops 1208180608 | bytes 11977216 | tf_op jit(solution)/shard_map/dot_general | solution.py:135
  42.4 0.4 convolution_convert_fusion.refs_0_
  42.8 2.9 %collective-permute-start = (bf16[288,512]{1,0:T(8,128)(2,1)S(1)}, bf16[288,512]{1,0:T(8,128)(2,1)S(1)}, u32[]{:S(2)}, u32[]{:S(2)}) collective-permute-start(bf16[288,512]{1,0:T(8,128)(2,1)S(1)} %convolution_convert_fusion.refs_0_), channel_id=1, source_target_pairs={{0,1},{1,2},{2,3},{3,4},{4,5},{5,6},{6,7},{7,0},{8,9},{9,10},{10,1... | collective-permute-start | bytes 884744 | tf_op jit(solution)/shard_map/ppermute | solution.py:96
  45.7 0.0 collective-permute-done.6
  45.8 3.8 %collective-permute-start.1 = (bf16[288,512]{1,0:T(8,128)(2,1)S(1)}, bf16[288,512]{1,0:T(8,128)(2,1)S(1)}, u32[]{:S(2)}, u32[]{:S(2)}) collective-permute-start(bf16[288,512]{1,0:T(8,128)(2,1)S(1)} %convolution_convert_fusion.refs_0_), channel_id=1, source_target_pairs={{0,7},{1,0},{2,1},{3,2},{4,3},{5,4},{6,5},{7,6},{8,15},{9,8},{10,9... | collective-permute-start | bytes 884744 | tf_op jit(solution)/shard_map/ppermute | solution.py:96
  49.6 4.8 %collective-permute-done.refs_1_ = bf16[288,512]{1,0:T(8,128)(2,1)S(1)} collective-permute-done((bf16[288,512]{1,0:T(8,128)(2,1)S(1)}, bf16[288,512]{1,0:T(8,128)(2,1)S(1)}, u32[]{:S(2)}, u32[]{:S(2)}) %collective-permute-start) | collective-permute-done | bytes 294944 | tf_op jit(solution)/shard_map/ppermute | solution.py:96
  54.4 1.9 %collective-permute-start.2 = (bf16[288,512]{1,0:T(8,128)(2,1)S(1)}, bf16[288,512]{1,0:T(8,128)(2,1)S(1)}, u32[]{:S(2)}, u32[]{:S(2)}) collective-permute-start(bf16[288,512]{1,0:T(8,128)(2,1)S(1)} %collective-permute-done.refs_1_), channel_id=1, source_target_pairs={{0,1},{1,2},{2,3},{3,4},{4,5},{5,6},{6,7},{7,0},{8,9},{9,10},{10,1... | collective-permute-start | bytes 884744 | tf_op jit(solution)/shard_map/ppermute | solution.py:96
  56.4 3.9 %collective-permute-start.7 = (bf16[576,256]{1,0:T(8,128)(2,1)S(1)}, bf16[576,256]{1,0:T(8,128)(2,1)S(1)}, u32[]{:S(2)}, u32[]{:S(2)}) collective-permute-start(bf16[576,256]{1,0:T(8,128)(2,1)S(1)} %pad_maximum_fusion), channel_id=1, source_target_pairs={{0,128},{64,192},{128,0},{192,64},{256,384},{320,448},{384,256},{4... | collective-permute-start | bytes 884744 | tf_op jit(solution)/shard_map/ppermute | solution.py:140
  60.3 0.0 collective-permute-done.1.refs_2_
  60.3 4.6 %collective-permute-start.3 = (bf16[288,512]{1,0:T(8,128)(2,1)S(1)}, bf16[288,512]{1,0:T(8,128)(2,1)S(1)}, u32[]{:S(2)}, u32[]{:S(2)}) collective-permute-start(bf16[288,512]{1,0:T(8,128)(2,1)S(1)} %collective-permute-done.1.refs_2_), channel_id=1, source_target_pairs={{0,7},{1,0},{2,1},{3,2},{4,3},{5,4},{6,5},{7,6},{8,15},{9,8},{10,9... | collective-permute-start | bytes 884744 | tf_op jit(solution)/shard_map/ppermute | solution.py:96
  64.9 0.1 collective-permute-done.2.refs_3_
  65.0 1.9 %collective-permute-start.4 = (bf16[288,512]{1,0:T(8,128)(2,1)S(1)}, bf16[288,512]{1,0:T(8,128)(2,1)S(1)}, u32[]{:S(2)}, u32[]{:S(2)}) collective-permute-start(bf16[288,512]{1,0:T(8,128)(2,1)S(1)} %collective-permute-done.2.refs_3_), channel_id=1, source_target_pairs={{0,1},{1,2},{2,3},{3,4},{4,5},{5,6},{6,7},{7,0},{8,9},{9,10},{10,1... | collective-permute-start | bytes 884744 | tf_op jit(solution)/shard_map/ppermute | solution.py:96
  66.9 0.0 collective-permute-done.7
  66.9 0.1 broadcast_select_fusion.1
  67.1 2.9 %collective-permute-done.3.refs_4_ = bf16[288,512]{1,0:T(8,128)(2,1)S(1)} collective-permute-done((bf16[288,512]{1,0:T(8,128)(2,1)S(1)}, bf16[288,512]{1,0:T(8,128)(2,1)S(1)}, u32[]{:S(2)}, u32[]{:S(2)}) %collective-permute-start.3) | collective-permute-done | bytes 294944 | tf_op jit(solution)/shard_map/ppermute | solution.py:96
  69.9 5.3 %collective-permute-start.5 = (bf16[288,512]{1,0:T(8,128)(2,1)S(1)}, bf16[288,512]{1,0:T(8,128)(2,1)S(1)}, u32[]{:S(2)}, u32[]{:S(2)}) collective-permute-start(bf16[288,512]{1,0:T(8,128)(2,1)S(1)} %collective-permute-done.3.refs_4_), channel_id=1, source_target_pairs={{0,7},{1,0},{2,1},{3,2},{4,3},{5,4},{6,5},{7,6},{8,15},{9,8},{10,9... | collective-permute-start | bytes 884744 | tf_op jit(solution)/shard_map/ppermute | solution.py:96
  75.2 0.0 collective-permute-done.4.refs_5_
  75.2 1.9 %collective-permute-start.8 = (bf16[288,512]{1,0:T(8,128)(2,1)S(1)}, bf16[288,512]{1,0:T(8,128)(2,1)S(1)}, u32[]{:S(2)}, u32[]{:S(2)}) collective-permute-start(bf16[288,512]{1,0:T(8,128)(2,1)S(1)} %collective-permute-done.4.refs_5_), channel_id=1, source_target_pairs={{0,1},{1,2},{2,3},{3,4},{4,5},{5,6},{6,7},{7,0},{8,9},{9,10},{10,1... | collective-permute-start | bytes 884744 | tf_op jit(solution)/shard_map/ppermute | solution.py:96
  77.2 1.5 %fusion.1 = bf16[576,512]{1,0:T(8,128)(2,1)} fusion(s32[576]{0:T(1024)S(1)} %fusion.31, bf16[576,256]{1,0:T(8,128)(2,1)S(1)} %get-tuple-element.22, bf16[576,256]{1,0:T(8,128)(2,1)S(1)} %get-tuple-element.21), kind=kOutput, calls=%fused_computation.2 | convolution fusion | flops 341544960 | bytes 1181952 | tf_op jit(solution)/shard_map/dot_general | solution.py:150
  78.7 4.6 %collective-permute-start.10 = (f32[576,128]{1,0:T(8,128)S(1)}, f32[576,128]{1,0:T(8,128)S(1)}, u32[]{:S(2)}, u32[]{:S(2)}) collective-permute-start(f32[576,128]{1,0:T(8,128)S(1)} %get-tuple-element.20), channel_id=1, source_target_pairs={{0,7},{1,0},{2,1},{3,2},{4,3},{5,4},{6,5},{7,6},{8,15},{9,8},{10,9... | collective-permute-start | bytes 884744 | tf_op jit(solution)/shard_map/ppermute | solution.py:96
  83.2 0.1 broadcast_select_fusion.4
  83.3 1.1 collective-permute-done.8.refs_0_
  84.4 0.0 all-to-all-done.1
  84.4 2.2 %shard_map.111 = f32[1,512]{1,0:T(1,128)S(1)} custom-call(bf16[288,512]{1,0:T(8,128)(2,1)S(1)} %collective-permute-done.8.refs_0_, bf16[8,72,512]{2,1,0:T(8,128)(2,1)} %bitcast.49, bf16[512,2048]{1,0:T(8,128)(2,1)} %bitcast.11.refs_14_.refs_2_), custom_call_target="tpu_custom_call" | custom-call | flops 603979776 | bytes 2392064 | tf_op jit(solution)/shard_map/pallas_call | solution.py:54
  86.6 0.0 copy-start.3
  86.7 0.0 copy-start.4
  86.7 0.0 copy-start.9
  86.7 0.0 copy-start.8
  86.7 0.0 copy-start.5
  86.7 0.0 copy-start.6
  86.7 0.0 collective-permute-done.5.refs_6_
  86.7 2.9 %shard_map.110 = f32[1,512]{1,0:T(1,128)S(1)} custom-call(bf16[288,512]{1,0:T(8,128)(2,1)S(1)} %convolution_convert_fusion.refs_0_, bf16[288,512]{1,0:T(8,128)(2,1)S(1)} %collective-permute-done.refs_1_, bf16[288,512]{1,0:T(8,128)(2,1)S(1)} %collective-permute-done.1.refs_2_, bf16[288,512]{1,0:T(8,128)(2,1)S(1)} %collective-permute-done.2.refs_3_, ...), custom_call_target="tpu_custom_call" | custom-call | flops 4227858432 | bytes 4161536 | tf_op jit(solution)/shard_map/pallas_call | solution.py:54
  89.7 0.6 broadcast_in_dim.67
  90.3 0.0 copy-done.3
  90.3 0.0 copy-done.4
  90.3 0.7 select_reduce_fusion
  92.8 0.0 copy-done.9
  92.8 0.2 fusion.15
  93.0 17.2 %all-to-all-start.2 = ((f32[32,2,128]{2,1,0:T(2,128)}), f32[32,2,128]{2,1,0:T(2,128)S(1)}, u32[]{:S(2)}, u32[]{:S(2)}) async-start(f32[32,2,128]{2,1,0:T(2,128)} %bitcast.13), calls=%async_computation.2 | async-start | bytes 65536 | tf_op jit(solution)/shard_map/all_to_all | solution.py:188
  110.3 0.0 copy-done.8
  110.3 0.8 fusion.9
  111.1 10.9 %all-to-all-done.2 = f32[32,2,128]{2,1,0:T(2,128)S(1)} async-done(((f32[32,2,128]{2,1,0:T(2,128)}), f32[32,2,128]{2,1,0:T(2,128)S(1)}, u32[]{:S(2)}, u32[]{:S(2)}) %all-to-all-start.2) | async-done | bytes 32800 | tf_op jit(solution)/shard_map/all_to_all | solution.py:188
  122.0 0.0 copy-done.5
  122.0 0.0 copy-done.6
  122.1 1.2 fusion.47
  123.3 1.9 %collective-permute-start.9 = (f32[1,128]{1,0:T(1,128)S(1)}, f32[1,128]{1,0:T(1,128)S(1)}, u32[]{:S(2)}, u32[]{:S(2)}) collective-permute-start(f32[1,128]{1,0:T(1,128)S(1)} %fusion.47), channel_id=1, source_target_pairs={{0,7},{1,0},{2,1},{3,2},{4,3},{5,4},{6,5},{7,6},{8,15},{9,8},{10,9... | collective-permute-start | bytes 1544 | tf_op jit(solution)/shard_map/ppermute | solution.py:96
  125.2 0.0 collective-permute-done.10
  125.2 2.4 %collective-permute-done.9 = f32[1,128]{1,0:T(1,128)S(1)} collective-permute-done((f32[1,128]{1,0:T(1,128)S(1)}, f32[1,128]{1,0:T(1,128)S(1)}, u32[]{:S(2)}, u32[]{:S(2)}) %collective-permute-start.9) | collective-permute-done | bytes 544 | tf_op jit(solution)/shard_map/ppermute | solution.py:96
  127.6 0.7 fusion.13
  (11 shorter events, 0.2 us)
Async XLA Ops:
  1.9 28.5 %all-to-all-start = ((bf16[12,24,512]{2,1,0:T(8,128)(2,1)}), bf16[12,24,512]{2,1,0:T(8,128)(2,1)S(1)}, u32[]{:S(2)}, u32[]{:S(2)}) async-start(bf16[12,24,512]{2,1,0:T(8,128)(2,1)} %bitcast.2), calls=%async_computation | async-start | bytes 589824 | tf_op jit(solution)/shard_map/all_to_all | solution.py:124
  15.7 1.6 %copy-start = (bf16[1,128,8192]{2,1,0:T(8,128)(2,1)S(1)}, bf16[1,128,8192]{2,1,0:T(8,128)(2,1)}, u32[]{:S(2)}) copy-start(bf16[1,128,8192]{2,1,0:T(8,128)(2,1)} %param.13) | copy-start | bytes 6291460
  19.3 15.9 %copy-start.2 = (bf16[1,128,576]{1,2,0:T(8,128)(2,1)S(1)}, bf16[1,128,576]{1,2,0:T(8,128)(2,1)}, u32[]{:S(2)}) copy-start(bf16[1,128,576]{1,2,0:T(8,128)(2,1)} %param.12) | copy-start | bytes 442372
  19.3 17.9 %copy-start.1 = (bf16[1,128,8192]{2,1,0:T(8,128)(2,1)S(1)}, bf16[1,128,8192]{2,1,0:T(8,128)(2,1)}, u32[]{:S(2)}) copy-start(bf16[1,128,8192]{2,1,0:T(8,128)(2,1)} %param.13) | copy-start | bytes 6291460
  19.3 17.9 %copy-start.7 = (bf16[1,128,576]{1,2,0:T(8,128)(2,1)S(1)}, bf16[1,128,576]{1,2,0:T(8,128)(2,1)}, u32[]{:S(2)}) copy-start(bf16[1,128,576]{1,2,0:T(8,128)(2,1)} %param.11) | copy-start | bytes 442372
  30.4 54.0 %all-to-all-start.1 = ((bf16[4,128,2048]{2,1,0:T(8,128)(2,1)}), bf16[4,128,2048]{2,1,0:T(8,128)(2,1)}, u32[]{:S(2)}, u32[]{:S(2)}) async-start(bf16[4,128,2048]{2,1,0:T(8,128)(2,1)} %shard_map.109), calls=%async_computation.1 | async-start | bytes 4194304 | tf_op jit(solution)/shard_map/all_to_all | solution.py:132
  35.2 10.5 %collective-permute-start.6 = (bf16[576,128]{1,0:T(8,128)(2,1)S(1)}, bf16[576,128]{1,0:T(8,128)(2,1)S(1)}, u32[]{:S(2)}, u32[]{:S(2)}) collective-permute-start(bf16[576,128]{1,0:T(8,128)(2,1)S(1)} %bitcast.59), channel_id=1, source_target_pairs={{0,64},{64,0},{128,192},{192,128},{256,320},{320,256},{384,448},{4... | collective-permute-start | bytes 442376 | tf_op jit(solution)/shard_map/ppermute | solution.py:140
  42.8 11.6 %collective-permute-start = (bf16[288,512]{1,0:T(8,128)(2,1)S(1)}, bf16[288,512]{1,0:T(8,128)(2,1)S(1)}, u32[]{:S(2)}, u32[]{:S(2)}) collective-permute-start(bf16[288,512]{1,0:T(8,128)(2,1)S(1)} %convolution_convert_fusion.refs_0_), channel_id=1, source_target_pairs={{0,1},{1,2},{2,3},{3,4},{4,5},{5,6},{6,7},{7,0},{8,9},{9,10},{10,1... | collective-permute-start | bytes 884744 | tf_op jit(solution)/shard_map/ppermute | solution.py:96
  45.8 14.6 %collective-permute-start.1 = (bf16[288,512]{1,0:T(8,128)(2,1)S(1)}, bf16[288,512]{1,0:T(8,128)(2,1)S(1)}, u32[]{:S(2)}, u32[]{:S(2)}) collective-permute-start(bf16[288,512]{1,0:T(8,128)(2,1)S(1)} %convolution_convert_fusion.refs_0_), channel_id=1, source_target_pairs={{0,7},{1,0},{2,1},{3,2},{4,3},{5,4},{6,5},{7,6},{8,15},{9,8},{10,9... | collective-permute-start | bytes 884744 | tf_op jit(solution)/shard_map/ppermute | solution.py:96
  54.4 10.6 %collective-permute-start.2 = (bf16[288,512]{1,0:T(8,128)(2,1)S(1)}, bf16[288,512]{1,0:T(8,128)(2,1)S(1)}, u32[]{:S(2)}, u32[]{:S(2)}) collective-permute-start(bf16[288,512]{1,0:T(8,128)(2,1)S(1)} %collective-permute-done.refs_1_), channel_id=1, source_target_pairs={{0,1},{1,2},{2,3},{3,4},{4,5},{5,6},{6,7},{7,0},{8,9},{9,10},{10,1... | collective-permute-start | bytes 884744 | tf_op jit(solution)/shard_map/ppermute | solution.py:96
  56.4 10.5 %collective-permute-start.7 = (bf16[576,256]{1,0:T(8,128)(2,1)S(1)}, bf16[576,256]{1,0:T(8,128)(2,1)S(1)}, u32[]{:S(2)}, u32[]{:S(2)}) collective-permute-start(bf16[576,256]{1,0:T(8,128)(2,1)S(1)} %pad_maximum_fusion), channel_id=1, source_target_pairs={{0,128},{64,192},{128,0},{192,64},{256,384},{320,448},{384,256},{4... | collective-permute-start | bytes 884744 | tf_op jit(solution)/shard_map/ppermute | solution.py:140
  60.3 9.6 %collective-permute-start.3 = (bf16[288,512]{1,0:T(8,128)(2,1)S(1)}, bf16[288,512]{1,0:T(8,128)(2,1)S(1)}, u32[]{:S(2)}, u32[]{:S(2)}) collective-permute-start(bf16[288,512]{1,0:T(8,128)(2,1)S(1)} %collective-permute-done.1.refs_2_), channel_id=1, source_target_pairs={{0,7},{1,0},{2,1},{3,2},{4,3},{5,4},{6,5},{7,6},{8,15},{9,8},{10,9... | collective-permute-start | bytes 884744 | tf_op jit(solution)/shard_map/ppermute | solution.py:96
  65.0 10.3 %collective-permute-start.4 = (bf16[288,512]{1,0:T(8,128)(2,1)S(1)}, bf16[288,512]{1,0:T(8,128)(2,1)S(1)}, u32[]{:S(2)}, u32[]{:S(2)}) collective-permute-start(bf16[288,512]{1,0:T(8,128)(2,1)S(1)} %collective-permute-done.2.refs_3_), channel_id=1, source_target_pairs={{0,1},{1,2},{2,3},{3,4},{4,5},{5,6},{6,7},{7,0},{8,9},{9,10},{10,1... | collective-permute-start | bytes 884744 | tf_op jit(solution)/shard_map/ppermute | solution.py:96
  69.9 16.8 %collective-permute-start.5 = (bf16[288,512]{1,0:T(8,128)(2,1)S(1)}, bf16[288,512]{1,0:T(8,128)(2,1)S(1)}, u32[]{:S(2)}, u32[]{:S(2)}) collective-permute-start(bf16[288,512]{1,0:T(8,128)(2,1)S(1)} %collective-permute-done.3.refs_4_), channel_id=1, source_target_pairs={{0,7},{1,0},{2,1},{3,2},{4,3},{5,4},{6,5},{7,6},{8,15},{9,8},{10,9... | collective-permute-start | bytes 884744 | tf_op jit(solution)/shard_map/ppermute | solution.py:96
  75.2 9.2 %collective-permute-start.8 = (bf16[288,512]{1,0:T(8,128)(2,1)S(1)}, bf16[288,512]{1,0:T(8,128)(2,1)S(1)}, u32[]{:S(2)}, u32[]{:S(2)}) collective-permute-start(bf16[288,512]{1,0:T(8,128)(2,1)S(1)} %collective-permute-done.4.refs_5_), channel_id=1, source_target_pairs={{0,1},{1,2},{2,3},{3,4},{4,5},{5,6},{6,7},{7,0},{8,9},{9,10},{10,1... | collective-permute-start | bytes 884744 | tf_op jit(solution)/shard_map/ppermute | solution.py:96
  78.7 46.5 %collective-permute-start.10 = (f32[576,128]{1,0:T(8,128)S(1)}, f32[576,128]{1,0:T(8,128)S(1)}, u32[]{:S(2)}, u32[]{:S(2)}) collective-permute-start(f32[576,128]{1,0:T(8,128)S(1)} %get-tuple-element.20), channel_id=1, source_target_pairs={{0,7},{1,0},{2,1},{3,2},{4,3},{5,4},{6,5},{7,6},{8,15},{9,8},{10,9... | collective-permute-start | bytes 884744 | tf_op jit(solution)/shard_map/ppermute | solution.py:96
  86.6 3.7 %copy-start.3 = (s32[12]{0:T(128)S(1)}, s32[12]{0:T(128)}, u32[]{:S(2)}) copy-start(s32[12]{0:T(128)} %param.21) | copy-start | bytes 148
  86.7 3.7 %copy-start.4 = (s32[12]{0:T(128)S(1)}, s32[12]{0:T(128)}, u32[]{:S(2)}) copy-start(s32[12]{0:T(128)} %param.20) | copy-start | bytes 148
  86.7 6.2 %copy-start.9 = (s32[12]{0:T(128)S(1)}, s32[12]{0:T(128)}, u32[]{:S(2)}) copy-start(s32[12]{0:T(128)} %param.19) | copy-start | bytes 148
  86.7 23.6 %copy-start.8 = (f32[12]{0:T(128)S(1)}, f32[12]{0:T(128)}, u32[]{:S(2)}) copy-start(f32[12]{0:T(128)} %param.18) | copy-start | bytes 148
  86.7 35.4 %copy-start.5 = (f32[1,128]{1,0:T(1,128)S(1)}, f32[1,128]{1,0:T(1,128)}, u32[]{:S(2)}) copy-start(f32[1,128]{1,0:T(1,128)} %param.14) | copy-start | bytes 1540
  86.7 35.3 %copy-start.6 = (f32[1,128]{1,0:T(1,128)S(1)}, f32[1,128]{1,0:T(1,128)}, u32[]{:S(2)}) copy-start(f32[1,128]{1,0:T(1,128)} %param.15) | copy-start | bytes 1540
  93.0 29.0 %all-to-all-start.2 = ((f32[32,2,128]{2,1,0:T(2,128)}), f32[32,2,128]{2,1,0:T(2,128)S(1)}, u32[]{:S(2)}, u32[]{:S(2)}) async-start(f32[32,2,128]{2,1,0:T(2,128)} %bitcast.13), calls=%async_computation.2 | async-start | bytes 65536 | tf_op jit(solution)/shard_map/all_to_all | solution.py:188
  123.3 4.3 %collective-permute-start.9 = (f32[1,128]{1,0:T(1,128)S(1)}, f32[1,128]{1,0:T(1,128)S(1)}, u32[]{:S(2)}, u32[]{:S(2)}) collective-permute-start(f32[1,128]{1,0:T(1,128)S(1)} %fusion.47), channel_id=1, source_target_pairs={{0,7},{1,0},{2,1},{3,2},{4,3},{5,4},{6,5},{7,6},{8,15},{9,8},{10,9... | collective-permute-start | bytes 1544 | tf_op jit(solution)/shard_map/ppermute | solution.py:96
